TPU v7x, 32 devices: a whole 2x2x4 slice. The times are simulated.
32 devices in a mesh: head: 4 (over z), frame: 8 (over y, x, core).
Axes of the slice: x: 2, y: 2, z: 4, core: 2. Of those that a mesh axis runs over, the one named last changes fastest.
Arguments:
- queries: bfloat16 [4096, 2048], P(('frame', 'head')), may hold values from -6 to 6
- key_states: bfloat16 [4096, 2048], P(('frame', 'head')), may hold values from -6 to 6
- value_states: bfloat16 [4096, 2048], P(('frame', 'head')), may hold values from -6 to 6
- attn_out: bfloat16 [4096, 2048], P(('frame', 'head')), may hold values from -6 to 6
- grad_out: bfloat16 [4096, 2048], P(('frame', 'head')), may hold values from -192 to 192
- frame_order: int32 [8], replicated, may hold values from 0 to 7, each once
- block_live: int32 [8, 4, 4], replicated, may hold values from 0 to 1, as said below
Outputs:
- grad_queries: bfloat16 [4096, 2048], P('frame', 'head')
- grad_keys: bfloat16 [4096, 2048], P('frame', 'head')
- grad_values: bfloat16 [4096, 2048], P('frame', 'head')
Inputs may be any that keep to these rules, and one draw needn't show every extreme that they name: `block_live`: every entry at distance 0 is 1; every entry at distances of 4 or more is 0.
All inputs are finite; a program needn't handle non-finite values.
Results may differ from a plain program's by a relative error of at most 0.0049.
Values may be sent and summed in bfloat16 or wider, within the bound.
No kernel may reach another device: no remote copies, remote signals or barrier semaphores. Data moves between devices by JAX's collectives and lax.ppermute only.
A program may use at most 128 MiB of HBM per device.

v0:
```python
import functools
import math

import jax
import jax.numpy as jnp
from jax import lax
from jax.experimental import pallas as pl
from jax.experimental.pallas import tpu as pltpu
from jax.sharding import PartitionSpec as P


HEADS = 16
HEAD_DIM = 128
NEG = -1e30
KEY_GROUP = 4
WIDE_GROUP = 6
TOGETHER = 4
REACH = 4
EXTRA = 8


VMEM = pl.BlockSpec(memory_space=pltpu.VMEM)
SMEM = pl.BlockSpec(memory_space=pltpu.SMEM)
HBM = pl.BlockSpec(memory_space=pltpu.HBM)
F32 = jnp.float32
BF16 = jnp.bfloat16
NT = (((1,), (1,)), ((), ()))
TN = (((0,), (0,)), ((), ()))
NN = (((1,), (0,)), ((), ()))


def dot(a, b, dims):
    return lax.dot_general(a, b, dims, preferred_element_type=F32)


def sds(shape, dtype):
    return jax.ShapeDtypeStruct(shape, dtype)


def lasts(microseconds):
    return pl.CostEstimate(flops=0, bytes_accessed=int(microseconds * 3.5e6), transcendentals=0)


def within(*shapes):
    held = sum(math.prod(s.shape) * s.dtype.itemsize for s in shapes)
    return pltpu.CompilerParams(vmem_limit_bytes=int(held * 5 // 4) + (6 << 20))


class Plan:
    def __init__(self, rows):
        self.nz = lax.axis_size("head")
        self.nf = lax.axis_size("frame")
        self.hh = HEADS // self.nz
        self.na = min(self.hh, self.nf)
        self.nb = self.nf // self.na
        self.rows = rows
        self.own = self.na * self.nz
        self.total = self.own * self.nb
        assert self.hh == self.na and rows == HEAD_DIM


def over_head(value, step):
    count = lax.axis_size("head")
    return lax.ppermute(value, "head", [(i, i ^ step) for i in range(count)])


def over_frame(value, step):
    count = lax.axis_size("frame")
    return lax.ppermute(value, "frame", [(i, i ^ step) for i in range(count)])


def bundles(plan, ids, refs, bufs, sems):
    width = plan.hh * HEAD_DIM
    out = []
    for r in range(plan.nz):
        cols = pl.ds(pl.multiple_of((ids[0] ^ r) * width, width), width)
        for w, (ref, buf) in enumerate(zip(refs, bufs)):
            out.append(pltpu.make_async_copy(ref.at[:, cols], buf.at[r], sems.at[w, r]))
    for copy in out:
        copy.start()
    return out


def within_bundle(ids, s):
    return pl.ds(pl.multiple_of((ids[1] ^ s) * HEAD_DIM, HEAD_DIM), HEAD_DIM)


def prep_kernel(plan, head_first, ids, x_ref, *refs):
    outs, buf, sems = refs[:-2], refs[-2], refs[-1]
    copies = bundles(plan, ids, [x_ref], [buf], sems)
    for r in range(plan.nz):
        copies[r].wait()
        for s in range(plan.na):
            piece = buf[r, :, within_bundle(ids, s)]
            if head_first:
                outs[r][s] = piece
            else:
                outs[s][r] = piece


def prep(plan, ids, x, head_first):
    pieces, chunk = (plan.nz, plan.na) if head_first else (plan.na, plan.nz)
    return pl.pallas_call(
        functools.partial(prep_kernel, plan, head_first),
        out_shape=[sds((chunk, plan.rows, HEAD_DIM), BF16)] * pieces,
        in_specs=[SMEM, HBM],
        out_specs=[VMEM] * pieces,
        scratch_shapes=[
            pltpu.VMEM((plan.nz, plan.rows, plan.hh * HEAD_DIM), BF16),
            pltpu.SemaphoreType.DMA((1, plan.nz)),
        ],
        cost_estimate=lasts(1.2),
        compiler_params=within(x, x),
    )(ids, x)


def prep_rest_kernel(plan, ids, g_ref, o_ref, v_ref, *refs):
    na, rows = plan.na, plan.rows
    outs, bufs, sems = refs[:na], refs[na : na + 3], refs[na + 3]
    copies = bundles(plan, ids, [g_ref, o_ref, v_ref], bufs, sems)
    ones = jnp.ones((EXTRA, HEAD_DIM), BF16)
    row = lax.broadcasted_iota(jnp.int32, (EXTRA, rows), 0)
    for r in range(plan.nz):
        for copy in copies[3 * r : 3 * r + 3]:
            copy.wait()
        for s in range(na):
            cols = within_bundle(ids, s)
            grad = bufs[0][r, :, cols]
            outs[s][r, :rows] = grad
            outs[s][r, rows + EXTRA :] = bufs[2][r, :, cols]
            product = grad.astype(F32) * bufs[1][r, :, cols].astype(F32)
            high = product.astype(BF16)
            low = (product - high.astype(F32)).astype(BF16)
            delta = dot(ones, high, NT) + dot(ones, low, NT)
            first = delta.astype(BF16).astype(F32)
            rest = delta - first
            second = rest.astype(BF16).astype(F32)
            parts = jnp.where(row == 2, rest - second, 0.0)
            parts = jnp.where(row == 0, first, jnp.where(row == 1, second, parts))
            outs[s][r, rows : rows + EXTRA] = parts.astype(BF16)


def prep_rest(plan, ids, g, o, v):
    return pl.pallas_call(
        functools.partial(prep_rest_kernel, plan),
        out_shape=[sds((plan.nz, 2 * plan.rows + EXTRA, HEAD_DIM), BF16)] * plan.na,
        in_specs=[SMEM] + [HBM] * 3,
        out_specs=[VMEM] * plan.na,
        scratch_shapes=[pltpu.VMEM((plan.nz, plan.rows, plan.hh * HEAD_DIM), BF16)] * 3
        + [pltpu.SemaphoreType.DMA((3, plan.nz))],
        cost_estimate=lasts(2),
        compiler_params=within(g, o, v, g, v),
        name="prep_rest",
    )(ids, g, o, v)


def lists_kernel(plan, ids, order, live_ref, by_key, n_key, query_of, numbers):
    nz, na, nb = plan.nz, plan.na, plan.nb
    z, a, b = ids[0], ids[1], ids[2]
    true = [z ^ r for r in range(nz)]

    def at_distance(d, carry):
        for rk in range(nz):
            count = jnp.int32(0)
            for r in range(nz):
                query_of[d * nz + rk, count] = jnp.int32(r)
                count = count + (live_ref[true[r], true[rk], d] > 0).astype(jnp.int32)
            numbers[d * nz + rk] = count
        return carry

    lax.fori_loop(1, REACH, at_distance, 0)

    def key_frame(s_key, carry):
        place_key = order[(a ^ s_key) * nb + b]

        def query_frame(ts, counts):
            t = ts // na
            place = order[(a ^ (ts - t * na)) * nb + (b ^ t)]
            d = jnp.abs(place - place_key)

            def found(counts):
                counts = list(counts)
                for rk in range(nz):
                    row = d * nz + rk
                    for u in range(nz):
                        by_key[s_key * nz + rk, counts[rk] + u] = ts * nz + query_of[row, u]
                    counts[rk] = counts[rk] + numbers[row]
                return tuple(counts)

            return lax.cond((d > 0) & (d < REACH), found, lambda counts: counts, counts)

        counts = lax.fori_loop(0, na * nb, query_frame, (jnp.int32(0),) * nz)
        for rk in range(nz):
            n_key[s_key * nz + rk] = counts[rk]
        return carry

    lax.fori_loop(0, na, key_frame, 0)


def lists(plan, ids, order, live):
    own, total, nz = plan.own, plan.total, plan.nz
    return pl.pallas_call(
        functools.partial(lists_kernel, plan),
        out_shape=[sds((own, total + WIDE_GROUP + nz), jnp.int32), sds((own,), jnp.int32)],
        in_specs=[SMEM] * 3,
        out_specs=[SMEM] * 2,
        scratch_shapes=[
            pltpu.SMEM((REACH * nz, nz), jnp.int32),
            pltpu.SMEM((REACH * nz,), jnp.int32),
        ],
        cost_estimate=lasts(3),
        compiler_params=within(),
        name="lists",
    )(ids, order, live)


def picks(table, row, count, first, size):
    out = []
    for u in range(size):
        valid = first + u < count
        out.append((jnp.where(valid, table[row, first + u], 0), valid))
    return out


def steps(count, size):
    return lax.div(count + (size - 1), size)


def totals_kernel(plan, by_key, n_key, k_ref, q_ref, out, peaks, sums):
    nz, na, own, rows, total = plan.nz, plan.na, plan.own, plan.rows, plan.total
    scale = HEAD_DIM**-0.5
    length = nz * rows
    peaks[own:, :] = jnp.full((peaks.shape[0] - own, rows), NEG, F32)
    sums[own:, :] = jnp.zeros((peaks.shape[0] - own, rows), F32)

    def near(s, carry):
        span = pl.ds(s * nz, nz)
        keys, q = k_ref[span].reshape(length, HEAD_DIM), q_ref[span].reshape(length, HEAD_DIM)
        scores = scale * dot(keys, q, NT)
        peak = jnp.max(scores, axis=0, keepdims=True)
        mass = jnp.sum(jnp.exp(scores - peak), axis=0, keepdims=True)
        for r in range(nz):
            peaks[pl.ds(s * nz + r, 1), :] = peak[:, r * rows : (r + 1) * rows]
            sums[pl.ds(s * nz + r, 1), :] = mass[:, r * rows : (r + 1) * rows]
        return carry

    lax.fori_loop(0, na, near, 0)

    def local(j, start):
        chosen = picks(by_key, j, n_key[j], start, WIDE_GROUP)
        places = [pl.ds(jnp.where(ok, i, total), 1) for i, ok in chosen]
        q = jnp.concatenate([q_ref[i] for i, _ in chosen], axis=0)
        scores = scale * dot(k_ref[j], q, NT)
        peak = jnp.max(scores, axis=0, keepdims=True)
        mass = jnp.sum(jnp.exp(scores - peak), axis=0, keepdims=True)
        return places, peak, mass

    def merge(places, peak, mass):
        old_peak = jnp.concatenate([peaks[place, :] for place in places], axis=1)
        old_mass = jnp.concatenate([sums[place, :] for place in places], axis=1)
        new_peak = jnp.maximum(old_peak, peak)
        new_mass = old_mass * jnp.exp(old_peak - new_peak) + mass * jnp.exp(peak - new_peak)
        for u, place in enumerate(places):
            peaks[place, :] = new_peak[:, u * rows : (u + 1) * rows]
            sums[place, :] = new_mass[:, u * rows : (u + 1) * rows]

    def away(m, carry):
        for found in [local(m * TOGETHER + u, 0) for u in range(TOGETHER)]:
            merge(*found)
        return carry

    lax.fori_loop(0, own // TOGETHER, away, 0)

    def rest(j, carry):
        def group(step, carry):
            merge(*local(j, step * WIDE_GROUP))
            return carry

        return lax.fori_loop(1, steps(n_key[j], WIDE_GROUP), group, carry)

    lax.fori_loop(0, own, rest, 0)
    peak = peaks[:total, :]
    out[...] = jnp.where(peak > 0.5 * NEG, peak + jnp.log(sums[:total, :]), NEG)


def totals(plan, by_key, n_key, keys, queries):
    return pl.pallas_call(
        functools.partial(totals_kernel, plan),
        out_shape=sds((plan.total, plan.rows), F32),
        in_specs=[SMEM, SMEM, VMEM, VMEM],
        out_specs=VMEM,
        scratch_shapes=[pltpu.VMEM((plan.total + 8, plan.rows), F32)] * 2,
        cost_estimate=lasts(6),
        compiler_params=within(keys, queries),
        name="totals",
    )(by_key, n_key, keys, queries)


def rows_kernel(plan, g_ref, *refs):
    nb, own, rows = plan.nb, plan.own, plan.rows
    parts, lse_all, delta_all = refs[:nb], refs[nb], refs[nb + 1]
    for t in range(nb):
        rivals = [parts[u][pl.ds((t ^ u) * own, own), :] for u in range(nb)]
        peak = functools.reduce(jnp.maximum, rivals)
        lse_all[pl.ds(t * own, own), :] = peak + jnp.log(sum(jnp.exp(x - peak) for x in rivals))

    def fill(i, carry):
        delta_all[pl.ds(i, 1), :] = jnp.sum(g_ref[i, rows:].astype(F32), axis=0, keepdims=True)
        return carry

    lax.fori_loop(0, plan.total, fill, 0)


def query_rows(plan, out_grads, parts):
    return pl.pallas_call(
        functools.partial(rows_kernel, plan),
        out_shape=[sds((plan.total, plan.rows), F32)] * 2,
        in_specs=[VMEM] * (1 + plan.nb),
        out_specs=[VMEM] * 2,
        cost_estimate=lasts(1),
        compiler_params=within(out_grads),
        name="query_rows",
    )(out_grads, *parts)


def grads_kernel(plan, span, first, last, by_key, n_key, q_ref, g_ref, lse_ref, delta_ref, k_ref, *refs):
    nz, na, nb, own, rows = plan.nz, plan.na, plan.nb, plan.own, plan.rows
    hd = HEAD_DIM
    scale = hd**-0.5
    length = nz * rows
    width = len(span)
    refs = list(refs)
    take = lambda n: [refs.pop(0) for _ in range(n)]
    v_refs = take(width)
    if not first:
        (dq_before,) = take(1)
    kv_outs = take(na)
    dq_outs = take(nb if last else 1)
    dk_all, dv_all = take(2)
    dq_all = refs.pop(0) if last else dq_outs[0]

    def begin(i, carry):
        dq_all[i] = jnp.zeros((rows, hd), F32) if first else dq_before[i]
        return carry

    lax.fori_loop(own if first else 0, plan.total, begin, 0)

    def wide_row(ref, start):
        return jnp.concatenate([ref[pl.ds(start + r, 1), :] for r in range(nz)], axis=1)

    def diagonal(s, carry):
        frame = pl.ds(s * nz, nz)
        k = jnp.concatenate([k_ref[s * nz + r] for r in span], axis=0)
        v = jnp.concatenate([v_ref[s] for v_ref in v_refs], axis=0)
        q, g = q_ref[frame].reshape(length, hd), g_ref[frame, :rows].reshape(length, hd)
        lse, delta = wide_row(lse_ref, s * nz), wide_row(delta_ref, s * nz)
        probs = jnp.exp(scale * dot(k, q, NT) - lse)
        dv = dot(probs.astype(BF16), g, NN)
        grad_scores = (probs * (dot(v, g, NT) - delta)).astype(BF16)
        dk = dot(grad_scores, q, NN)
        dq = dot(grad_scores, k, TN).reshape(nz, rows, hd)
        for x in range(width):
            dv_all[s * width + x] = dv[x * rows : (x + 1) * rows]
            dk_all[s * width + x] = dk[x * rows : (x + 1) * rows]
        if first:
            dq_all[frame] = dq
        else:
            dq_all[frame] += dq
        return carry

    lax.fori_loop(0, na, diagonal, 0)

    def terms(s, x, j, start):
        k, v = k_ref[j], v_refs[x][s]
        chosen = picks(by_key, j, n_key[j], start, KEY_GROUP)
        q = jnp.concatenate([q_ref[i] for i, _ in chosen], axis=0)
        g = jnp.concatenate([g_ref[i, :rows] for i, _ in chosen], axis=0)
        lse = jnp.concatenate([jnp.where(ok, lse_ref[pl.ds(i, 1), :], -NEG) for i, ok in chosen], axis=1)
        delta = jnp.concatenate([delta_ref[pl.ds(i, 1), :] for i, _ in chosen], axis=1)
        probs = jnp.exp(scale * dot(k, q, NT) - lse)
        dv = dot(probs.astype(BF16), g, NN)
        grad_scores = (probs * (dot(v, g, NT) - delta)).astype(BF16)
        dk = dot(grad_scores, q, NN)
        return chosen, dv, dk, dot(grad_scores, k, TN)

    def add(s, x, found):
        chosen, dv, dk, dq = found
        dv_all[s * width + x] += dv
        dk_all[s * width + x] += dk
        for u, (i, _) in enumerate(chosen):
            dq_all[i] += dq[u * rows : (u + 1) * rows]

    def away(s, carry):
        for x, found in [(x, terms(s, x, s * nz + r, 0)) for x, r in enumerate(span)]:
            add(s, x, found)
        for x, r in enumerate(span):

            def group(step, carry, x=x, r=r):
                add(s, x, terms(s, x, s * nz + r, step * KEY_GROUP))
                return carry

            lax.fori_loop(1, steps(n_key[s * nz + r], KEY_GROUP), group, 0)
        return carry

    lax.fori_loop(0, na, away, 0)

    for s, out in enumerate(kv_outs):
        for x in range(width):
            out[0, x] = (scale * dk_all[s * width + x]).astype(BF16)
            out[1, x] = dv_all[s * width + x].astype(BF16)
    if last:
        for t in range(nb):

            def drain(m, carry, t=t):
                dq_outs[t][m] = scale * dq_all[t * own + m]
                return carry

            lax.fori_loop(0, own, drain, 0)


def grads(plan, span, tables, queries, out_grads, lse, delta, keys, values, dq_before, last):
    nb, na, own, rows, total = plan.nb, plan.na, plan.own, plan.rows, plan.total
    hd, width, first = HEAD_DIM, len(span), dq_before is None
    kv = [sds((2, width, rows, hd), BF16)] * na
    dq = [sds((own, rows, hd), F32)] * nb if last else [sds((total, rows, hd), F32)]
    before = [] if first else [dq_before]
    partial = sds((own, rows, hd), F32)
    outs = pl.pallas_call(
        functools.partial(grads_kernel, plan, span, first, last),
        out_shape=kv + dq,
        in_specs=[SMEM] * 2 + [VMEM] * (5 + width + len(before)),
        out_specs=[VMEM] * (na + len(dq)),
        scratch_shapes=[pltpu.VMEM((na * width, rows, hd), F32)] * 2
        + ([pltpu.VMEM((total, rows, hd), F32)] if last else []),
        cost_estimate=lasts(7),
        compiler_params=within(queries, out_grads, keys, keys, *[partial] * (4 + 3 * nb)),
    )(*tables, queries, out_grads, lse, delta, keys, *values, *before)
    return outs[:na], outs[na:]


def pack_kernel(plan, *refs):
    nb, nz = plan.nb, plan.nz
    for s, out in enumerate(refs[nb:]):
        for r in range(nz):
            out[0, r] = sum(ref[s * nz + r] for ref in refs[:nb]).astype(BF16)


def pack(plan, partials):
    return pl.pallas_call(
        functools.partial(pack_kernel, plan),
        out_shape=[sds((1, plan.nz, plan.rows, HEAD_DIM), BF16)] * plan.na,
        in_specs=[VMEM] * plan.nb,
        out_specs=[VMEM] * plan.na,
        cost_estimate=lasts(1),
        compiler_params=within(*partials, *partials),
        name="pack",
    )(*partials)


def assemble_kernel(plan, spans, n, ids, *refs):
    na, rows, hd = plan.na, plan.rows, HEAD_DIM
    refs = list(refs)
    outs = refs[na * len(spans) :]
    for span in spans:
        for s in range(na):
            piece = refs.pop(0)
            cols = pl.ds(pl.multiple_of((ids[1] ^ s) * hd, hd), hd)
            for w in range(n):
                for x, r in enumerate(span):
                    place = pl.ds(pl.multiple_of((ids[0] ^ r) * rows, rows), rows)
                    outs[w][place, cols] = piece[w, x]


def assemble(plan, ids, spans, groups):
    n = groups[0][0].shape[0]
    pieces = [piece for group in groups for piece in group]
    return pl.pallas_call(
        functools.partial(assemble_kernel, plan, spans, n),
        out_shape=[sds((plan.nz * plan.rows, plan.na * HEAD_DIM), BF16)] * n,
        in_specs=[SMEM] + [VMEM] * len(pieces),
        out_specs=[VMEM] * n,
        cost_estimate=lasts(1.5),
        compiler_params=within(*pieces, *pieces),
    )(ids, *pieces)


def local(queries, key_states, value_states, attn_out, grad_out, frame_order, block_live):
    plan = Plan(queries.shape[0])
    nz, na, nb = plan.nz, plan.na, plan.nb
    slot = lax.axis_index("frame")
    ids = jnp.stack([lax.axis_index("head"), slot // nb, slot % nb]).astype(jnp.int32)

    def staged(order, pieces, send):
        moved = {}
        for step in order:
            moved[step] = send(pieces[step], step)
        return [pieces[0]] + [moved[step] for step in range(1, len(pieces))]

    def head_stage(pieces):
        return staged([*range(2, nz), 1], pieces, over_head)

    def frame_stage(pieces):
        return staged(range(na - 1, 0, -1), pieces, lambda x, s: over_frame(x, s * nb))

    def swapped(parts):
        return staged(range(1, nb), parts, over_frame)

    def regroup(pieces):
        return [jnp.concatenate([p[i : i + 1] for p in pieces]) for i in range(pieces[0].shape[0])]

    def flat_frames_first(by_frame):
        return jnp.concatenate(by_frame)

    def flat_heads_first(by_head):
        return jnp.concatenate([p[s : s + 1] for s in range(na) for p in by_head])

    q_sent = head_stage(prep(plan, ids, queries, True))
    k_near = frame_stage(prep(plan, ids, key_states, False))
    gv_near = frame_stage(prep_rest(plan, ids, grad_out, attn_out, value_states))
    by_key, n_key = lists(plan, ids, frame_order, block_live.transpose(1, 2, 0))
    keys = flat_heads_first(head_stage(regroup(k_near)))
    q_own = flat_frames_first(frame_stage(regroup(q_sent)))
    q_all = jnp.concatenate(swapped([q_own] * nb))
    g_own = flat_heads_first(head_stage(regroup([p[:, : plan.rows + EXTRA] for p in gv_near])))
    g_all = jnp.concatenate(swapped([g_own] * nb))
    values = head_stage(regroup([p[:, plan.rows + EXTRA :] for p in gv_near]))

    lse_part = totals(plan, by_key, n_key, keys, q_all)
    lse, delta = query_rows(plan, g_all, swapped([lse_part] * nb))
    spans = [range(0, 2), range(2, nz)]
    kv_home, dq = [], None
    for place, span in enumerate(spans):
        last = place == len(spans) - 1
        kv, dq_parts = grads(
            plan, span, (by_key, n_key), q_all, g_all, lse, delta, keys,
            [values[r] for r in span], dq, last,
        )
        dq = dq_parts[0]
        kv_home.append(frame_stage(kv))
    dq_home = frame_stage(pack(plan, swapped(dq_parts)))
    grad_key, grad_value = assemble(plan, ids, spans, kv_home)
    (grad_query,) = assemble(plan, ids, [range(nz)], [dq_home])
    return grad_query, grad_key, grad_value


def solution(mesh):
    rows = P(("frame", "head"), None)
    in_specs = (rows,) * 5 + (P(), P())
    out_specs = (P("frame", "head"),) * 3
    return jax.shard_map(local, mesh=mesh, in_specs=in_specs, out_specs=out_specs, check_vma=False)
```

profile of v0, /device:TPU:0, one launch (start us, length us, event | category | flops | bytes accessed | tf_op | source)
XLA Modules:
  0.0 121.6 jit_solution(1794426018621880576)
XLA Ops:
  0.6 0.1 pad_add_fusion.ids
  0.7 1.0 copy-done
  1.8 0.8 shard_map.94
  2.6 3.1 %collective-permute-start = (bf16[4,128,128]{2,1,0:T(8,128)(2,1)S(1)}, bf16[4,128,128]{2,1,0:T(8,128)(2,1)S(1)}, u32[]{:S(2)}, u32[]{:S(2)}) collective-permute-start(bf16[4,128,128]{2,1,0:T(8,128)(2,1)S(1)} %get-tuple-element.39), channel_id=1, source_target_pairs={{0,8},{8,0},{16,24},{24,16},{1,9},{9,1},{17,25},{25,17},{2,10},{10... | collective-permute-start | bytes 393224 | tf_op jit(solution)/shard_map/ppermute | solution.py:64
  5.7 2.6 %collective-permute-start.1 = (bf16[4,128,128]{2,1,0:T(8,128)(2,1)S(1)}, bf16[4,128,128]{2,1,0:T(8,128)(2,1)S(1)}, u32[]{:S(2)}, u32[]{:S(2)}) collective-permute-start(bf16[4,128,128]{2,1,0:T(8,128)(2,1)S(1)} %get-tuple-element.40), channel_id=1, source_target_pairs={{0,16},{8,24},{16,0},{24,8},{1,17},{9,25},{17,1},{25,9},{2,18},{10... | collective-permute-start | bytes 393224 | tf_op jit(solution)/shard_map/ppermute | solution.py:64
  8.3 1.0 copy-done.1
  9.3 0.8 shard_map.95
  10.1 1.8 %collective-permute-start.14 = (bf16[4,128,128]{2,1,0:T(8,128)(2,1)S(1)}, bf16[4,128,128]{2,1,0:T(8,128)(2,1)S(1)}, u32[]{:S(2)}, u32[]{:S(2)}) collective-permute-start(bf16[4,128,128]{2,1,0:T(8,128)(2,1)S(1)} %get-tuple-element.47), channel_id=1, source_target_pairs={{0,2},{1,3},{2,0},{3,1},{4,6},{5,7},{6,4},{7,5},{8,10},{9,11},{10,... | collective-permute-start | bytes 393224 | tf_op jit(solution)/shard_map/ppermute | solution.py:69
  11.9 1.5 %collective-permute-start.15 = (bf16[4,128,128]{2,1,0:T(8,128)(2,1)S(1)}, bf16[4,128,128]{2,1,0:T(8,128)(2,1)S(1)}, u32[]{:S(2)}, u32[]{:S(2)}) collective-permute-start(bf16[4,128,128]{2,1,0:T(8,128)(2,1)S(1)} %get-tuple-element.48), channel_id=1, source_target_pairs={{0,4},{1,5},{2,6},{3,7},{4,0},{5,1},{6,2},{7,3},{8,12},{9,13},{10,... | collective-permute-start | bytes 393224 | tf_op jit(solution)/shard_map/ppermute | solution.py:69
  13.4 1.0 copy-done.3
  14.4 1.0 copy-done.4
  15.5 2.1 %prep_rest.1 = (bf16[4,264,128]{2,1,0:T(8,128)(2,1)S(1)}, bf16[4,264,128]{2,1,0:T(8,128)(2,1)S(1)}, bf16[4,264,128]{2,1,0:T(8,128)(2,1)S(1)}, bf16[4,264,128]{2,1,0:T(8,128)(2,1)S(1)}) custom-call(s32[3]{0:T(128)S(1)} %pad_add_fusion.ids, bf16[128,2048]{1,0:T(8,128)(2,1)S(1)} %copy-done.2, bf16[128,2048]{1,0:T(8,128)(2,1)S(1)} %copy-done.3, ...), custom_call_target="tpu_custom_call" | custom-call | bytes 7000000 | tf_op jit(solution)/shard_map/prep_rest/pallas_call | solution.py:144
  17.7 3.5 %lists.1 = (s32[16,42]{1,0:T(8,128)S(1)}, s32[16]{0:T(128)S(1)}) custom-call(s32[3]{0:T(128)S(1)} %pad_add_fusion.ids, s32[8]{0:T(128)S(1)} %copy-done.6, s32[4,4,8]{2,1,0:T(4,128)S(1)} %bitcast.4), custom_call_target="tpu_custom_call" | custom-call | bytes 10500000 | tf_op jit(solution)/shard_map/lists/pallas_call | solution.py:202
  21.2 0.3 collective-permute-start.16
  21.5 1.8 %collective-permute-start.7 = (bf16[4,264,128]{2,1,0:T(8,128)(2,1)S(1)}, bf16[4,264,128]{2,1,0:T(8,128)(2,1)S(1)}, u32[]{:S(2)}, u32[]{:S(2)}) collective-permute-start(bf16[4,264,128]{2,1,0:T(8,128)(2,1)S(1)} %get-tuple-element.43), channel_id=1, source_target_pairs={{0,2},{1,3},{2,0},{3,1},{4,6},{5,7},{6,4},{7,5},{8,10},{9,11},{10,... | collective-permute-start | bytes 811016 | tf_op jit(solution)/shard_map/ppermute | solution.py:69
  23.3 1.6 %collective-permute-start.8 = (bf16[4,264,128]{2,1,0:T(8,128)(2,1)S(1)}, bf16[4,264,128]{2,1,0:T(8,128)(2,1)S(1)}, u32[]{:S(2)}, u32[]{:S(2)}) collective-permute-start(bf16[4,264,128]{2,1,0:T(8,128)(2,1)S(1)} %get-tuple-element.44), channel_id=1, source_target_pairs={{0,4},{1,5},{2,6},{3,7},{4,0},{5,1},{6,2},{7,3},{8,12},{9,13},{10,... | collective-permute-start | bytes 811016 | tf_op jit(solution)/shard_map/ppermute | solution.py:69
  24.9 3.6 %collective-permute-done.16 = bf16[4,128,128]{2,1,0:T(8,128)(2,1)S(1)} collective-permute-done((bf16[4,128,128]{2,1,0:T(8,128)(2,1)S(1)}, bf16[4,128,128]{2,1,0:T(8,128)(2,1)S(1)}, u32[]{:S(2)}, u32[]{:S(2)}) %collective-permute-start.16) | collective-permute-done | bytes 131104 | tf_op jit(solution)/shard_map/ppermute | solution.py:69
  28.5 0.3 collective-permute-start.9
  28.8 1.0 collective-permute-start.17
  29.9 1.6 %collective-permute-start.3 = (bf16[4,128,128]{2,1,0:T(8,128)(2,1)S(1)}, bf16[4,128,128]{2,1,0:T(8,128)(2,1)S(1)}, u32[]{:S(2)}, u32[]{:S(2)}) collective-permute-start(bf16[4,128,128]{2,1,0:T(8,128)(2,1)S(1)} %pad_maximum_fusion.3), channel_id=1, source_target_pairs={{0,2},{1,3},{2,0},{3,1},{4,6},{5,7},{6,4},{7,5},{8,10},{9,11},{10,... | collective-permute-start | bytes 393224 | tf_op jit(solution)/shard_map/ppermute | solution.py:69
  31.5 2.3 %collective-permute-done.17 = bf16[4,128,128]{2,1,0:T(8,128)(2,1)S(1)} collective-permute-done((bf16[4,128,128]{2,1,0:T(8,128)(2,1)S(1)}, bf16[4,128,128]{2,1,0:T(8,128)(2,1)S(1)}, u32[]{:S(2)}, u32[]{:S(2)}) %collective-permute-start.17) | collective-permute-done | bytes 131104 | tf_op jit(solution)/shard_map/ppermute | solution.py:64
  33.9 1.7 %collective-permute-start.4 = (bf16[4,128,128]{2,1,0:T(8,128)(2,1)S(1)}, bf16[4,128,128]{2,1,0:T(8,128)(2,1)S(1)}, u32[]{:S(2)}, u32[]{:S(2)}) collective-permute-start(bf16[4,128,128]{2,1,0:T(8,128)(2,1)S(1)} %pad_maximum_fusion.4), channel_id=1, source_target_pairs={{0,4},{1,5},{2,6},{3,7},{4,0},{5,1},{6,2},{7,3},{8,12},{9,13},{10,... | collective-permute-start | bytes 393224 | tf_op jit(solution)/shard_map/ppermute | solution.py:69
  35.6 3.9 %collective-permute-done.3 = bf16[4,128,128]{2,1,0:T(8,128)(2,1)S(1)} collective-permute-done((bf16[4,128,128]{2,1,0:T(8,128)(2,1)S(1)}, bf16[4,128,128]{2,1,0:T(8,128)(2,1)S(1)}, u32[]{:S(2)}, u32[]{:S(2)}) %collective-permute-start.3) | collective-permute-done | bytes 131104 | tf_op jit(solution)/shard_map/ppermute | solution.py:69
  39.5 1.5 %collective-permute-start.5 = (bf16[4,128,128]{2,1,0:T(8,128)(2,1)S(1)}, bf16[4,128,128]{2,1,0:T(8,128)(2,1)S(1)}, u32[]{:S(2)}, u32[]{:S(2)}) collective-permute-start(bf16[4,128,128]{2,1,0:T(8,128)(2,1)S(1)} %pad_maximum_fusion.5), channel_id=1, source_target_pairs={{0,6},{1,7},{2,4},{3,5},{4,2},{5,3},{6,0},{7,1},{8,14},{9,15},{10,... | collective-permute-start | bytes 393224 | tf_op jit(solution)/shard_map/ppermute | solution.py:69
  41.0 0.1 constant_dynamic-update-slice_fusion.2
  41.0 1.7 %collective-permute-start.18 = (bf16[4,128,128]{2,1,0:T(8,128)(2,1)S(1)}, bf16[4,128,128]{2,1,0:T(8,128)(2,1)S(1)}, u32[]{:S(2)}, u32[]{:S(2)}) collective-permute-start(bf16[4,128,128]{2,1,0:T(8,128)(2,1)S(1)} %pad_maximum_fusion.7), channel_id=1, source_target_pairs={{0,16},{8,24},{16,0},{24,8},{1,17},{9,25},{17,1},{25,9},{2,18},{10... | collective-permute-start | bytes 393224 | tf_op jit(solution)/shard_map/ppermute | solution.py:64
  42.8 2.6 %collective-permute-done.5 = bf16[4,128,128]{2,1,0:T(8,128)(2,1)S(1)} collective-permute-done((bf16[4,128,128]{2,1,0:T(8,128)(2,1)S(1)}, bf16[4,128,128]{2,1,0:T(8,128)(2,1)S(1)}, u32[]{:S(2)}, u32[]{:S(2)}) %collective-permute-start.5) | collective-permute-done | bytes 131104 | tf_op jit(solution)/shard_map/ppermute | solution.py:69
  45.4 3.5 %collective-permute-start.19 = (bf16[4,128,128]{2,1,0:T(8,128)(2,1)S(1)}, bf16[4,128,128]{2,1,0:T(8,128)(2,1)S(1)}, u32[]{:S(2)}, u32[]{:S(2)}) collective-permute-start(bf16[4,128,128]{2,1,0:T(8,128)(2,1)S(1)} %pad_maximum_fusion.8), channel_id=1, source_target_pairs={{0,24},{8,16},{16,8},{24,0},{1,25},{9,17},{17,9},{25,1},{2,26},{10... | collective-permute-start | bytes 393224 | tf_op jit(solution)/shard_map/ppermute | solution.py:64
  49.0 1.4 %collective-permute-done.18 = bf16[4,128,128]{2,1,0:T(8,128)(2,1)S(1)} collective-permute-done((bf16[4,128,128]{2,1,0:T(8,128)(2,1)S(1)}, bf16[4,128,128]{2,1,0:T(8,128)(2,1)S(1)}, u32[]{:S(2)}, u32[]{:S(2)}) %collective-permute-start.18) | collective-permute-done | bytes 131104 | tf_op jit(solution)/shard_map/ppermute | solution.py:64
  50.4 1.8 %collective-permute-done.19 = bf16[4,128,128]{2,1,0:T(8,128)(2,1)S(1)} collective-permute-done((bf16[4,128,128]{2,1,0:T(8,128)(2,1)S(1)}, bf16[4,128,128]{2,1,0:T(8,128)(2,1)S(1)}, u32[]{:S(2)}, u32[]{:S(2)}) %collective-permute-start.19) | collective-permute-done | bytes 131104 | tf_op jit(solution)/shard_map/ppermute | solution.py:64
  52.5 1.6 %collective-permute-start.10 = (bf16[4,136,128]{2,1,0:T(8,128)(2,1)S(1)}, bf16[4,136,128]{2,1,0:T(8,128)(2,1)S(1)}, u32[]{:S(2)}, u32[]{:S(2)}) collective-permute-start(bf16[4,136,128]{2,1,0:T(8,128)(2,1)S(1)} %pad_maximum_fusion), channel_id=1, source_target_pairs={{0,8},{8,0},{16,24},{24,16},{1,9},{9,1},{17,25},{25,17},{2,10},{10... | collective-permute-start | bytes 417800 | tf_op jit(solution)/shard_map/ppermute | solution.py:64
  54.2 2.5 %collective-permute-start.11 = (bf16[4,136,128]{2,1,0:T(8,128)(2,1)S(1)}, bf16[4,136,128]{2,1,0:T(8,128)(2,1)S(1)}, u32[]{:S(2)}, u32[]{:S(2)}) collective-permute-start(bf16[4,136,128]{2,1,0:T(8,128)(2,1)S(1)} %pad_maximum_fusion.1), channel_id=1, source_target_pairs={{0,16},{8,24},{16,0},{24,8},{1,17},{9,25},{17,1},{25,9},{2,18},{10... | collective-permute-start | bytes 417800 | tf_op jit(solution)/shard_map/ppermute | solution.py:64
  56.7 0.4 collective-permute-start.12
  57.2 1.2 collective-permute-done.10
  58.4 7.1 %collective-permute-done.11 = bf16[4,136,128]{2,1,0:T(8,128)(2,1)S(1)} collective-permute-done((bf16[4,136,128]{2,1,0:T(8,128)(2,1)S(1)}, bf16[4,136,128]{2,1,0:T(8,128)(2,1)S(1)}, u32[]{:S(2)}, u32[]{:S(2)}) %collective-permute-start.11) | collective-permute-done | bytes 139296 | tf_op jit(solution)/shard_map/ppermute | solution.py:64
  65.8 0.1 collective-permute-start.13
  65.9 3.0 %collective-permute-start.21 = (bf16[4,128,128]{2,1,0:T(8,128)(2,1)S(1)}, bf16[4,128,128]{2,1,0:T(8,128)(2,1)S(1)}, u32[]{:S(2)}, u32[]{:S(2)}) collective-permute-start(bf16[4,128,128]{2,1,0:T(8,128)(2,1)S(1)} %pad_maximum_fusion.9), channel_id=1, source_target_pairs={{0,16},{8,24},{16,0},{24,8},{1,17},{9,25},{17,1},{25,9},{2,18},{10... | collective-permute-start | bytes 393224 | tf_op jit(solution)/shard_map/ppermute | solution.py:64
  68.9 1.5 %collective-permute-start.22 = (bf16[4,128,128]{2,1,0:T(8,128)(2,1)S(1)}, bf16[4,128,128]{2,1,0:T(8,128)(2,1)S(1)}, u32[]{:S(2)}, u32[]{:S(2)}) collective-permute-start(bf16[4,128,128]{2,1,0:T(8,128)(2,1)S(1)} %pad_maximum_fusion.10), channel_id=1, source_target_pairs={{0,24},{8,16},{16,8},{24,0},{1,25},{9,17},{17,9},{25,1},{2,26},{10... | collective-permute-start | bytes 393224 | tf_op jit(solution)/shard_map/ppermute | solution.py:64
  70.4 0.1 collective-permute-start.23
  70.6 0.1 constant_dynamic-update-slice_fusion.7.q_ref
  70.6 5.8 %totals.1.refs_0_ = f32[32,128]{1,0:T(8,128)S(1)} custom-call(s32[16,42]{1,0:T(8,128)S(1)} %get-tuple-element.36.by_key, s32[16]{0:T(128)S(1)} %get-tuple-element.37.n_key, bf16[16,128,128]{2,1,0:T(8,128)(2,1)S(1)} %constant_dynamic-update-slice_fusion.48.k_ref, bf16[32,128,128]{2,1,0:T(8,128)(2,1)S(1)} %constant_dynamic-update-slice_fusion.7.q_ref), custom_call_target="tpu_custom_call" | custom-call | bytes 21000000 | tf_op jit(solution)/shard_map/totals/pallas_call | solution.py:287
  76.4 0.1 collective-permute-start.20
  76.5 0.1 constant_dynamic-update-slice_fusion.31.g_ref
  76.6 1.1 collective-permute-done.20.refs_1_
  77.7 0.3 query_rows.1
  78.0 2.2 %collective-permute-done.23.refs_1_ = bf16[4,128,128]{2,1,0:T(8,128)(2,1)S(1)} collective-permute-done((bf16[4,128,128]{2,1,0:T(8,128)(2,1)S(1)}, bf16[4,128,128]{2,1,0:T(8,128)(2,1)S(1)}, u32[]{:S(2)}, u32[]{:S(2)}) %collective-permute-start.23) | collective-permute-done | bytes 131104 | tf_op jit(solution)/shard_map/ppermute | solution.py:64
  80.2 8.7 %shard_map.96 = (bf16[2,2,128,128]{3,2,1,0:T(8,128)(2,1)S(1)}, bf16[2,2,128,128]{3,2,1,0:T(8,128)(2,1)S(1)}, bf16[2,2,128,128]{3,2,1,0:T(8,128)(2,1)S(1)}, bf16[...) custom-call(s32[16,42]{1,0:T(8,128)S(1)} %get-tuple-element.36.by_key, s32[16]{0:T(128)S(1)} %get-tuple-element.37.n_key, ...), custom_call_target="tpu_custom_call" | custom-call | bytes 24500000 | tf_op jit(solution)/shard_map/pallas_call | solution.py:428
  88.9 9.1 %shard_map.97 = (bf16[2,2,128,128]{3,2,1,0:T(8,128)(2,1)S(1)}, bf16[2,2,128,128]{3,2,1,0:T(8,128)(2,1)S(1)}, bf16[2,2,128,128]{3,2,1,0:T(8,128)(2,1)S(1)}, bf16[...) custom-call(s32[16,42]{1,0:T(8,128)S(1)} %get-tuple-element.36.by_key, ...), custom_call_target="tpu_custom_call" | custom-call | bytes 24500000 | tf_op jit(solution)/shard_map/pallas_call | solution.py:428
  98.0 0.1 collective-permute-start.24
  98.1 2.5 %collective-permute-start.31 = (bf16[2,2,128,128]{3,2,1,0:T(8,128)(2,1)S(1)}, bf16[2,2,128,128]{3,2,1,0:T(8,128)(2,1)S(1)}, u32[]{:S(2)}, u32[]{:S(2)}) collective-permute-start(bf16[2,2,128,128]{3,2,1,0:T(8,128)(2,1)S(1)} %get-tuple-element.64), channel_id=1, source_target_pairs={{0,2},{1,3},{2,0},{3,1},{4,6},{5,7},{6,4},{7,5},{8,10},{9,11},{10,... | collective-permute-start | bytes 393224 | tf_op jit(solution)/shard_map/ppermute | solution.py:69
  100.6 1.5 %collective-permute-start.33 = (bf16[2,2,128,128]{3,2,1,0:T(8,128)(2,1)S(1)}, bf16[2,2,128,128]{3,2,1,0:T(8,128)(2,1)S(1)}, u32[]{:S(2)}, u32[]{:S(2)}) collective-permute-start(bf16[2,2,128,128]{3,2,1,0:T(8,128)(2,1)S(1)} %get-tuple-element.66), channel_id=1, source_target_pairs={{0,6},{1,7},{2,4},{3,5},{4,2},{5,3},{6,0},{7,1},{8,14},{9,15},{10,... | collective-permute-start | bytes 393224 | tf_op jit(solution)/shard_map/ppermute | solution.py:69
  102.1 1.9 %collective-permute-start.28 = (bf16[2,2,128,128]{3,2,1,0:T(8,128)(2,1)S(1)}, bf16[2,2,128,128]{3,2,1,0:T(8,128)(2,1)S(1)}, u32[]{:S(2)}, u32[]{:S(2)}) collective-permute-start(bf16[2,2,128,128]{3,2,1,0:T(8,128)(2,1)S(1)} %get-tuple-element.60), channel_id=1, source_target_pairs={{0,2},{1,3},{2,0},{3,1},{4,6},{5,7},{6,4},{7,5},{8,10},{9,11},{10,... | collective-permute-start | bytes 393224 | tf_op jit(solution)/shard_map/ppermute | solution.py:69
  104.1 0.2 pack.1
  104.3 0.6 collective-permute-done.31.refs_5_
  104.8 1.0 collective-permute-start.30
  105.9 3.8 %collective-permute-done.32.refs_6_ = bf16[2,2,128,128]{3,2,1,0:T(8,128)(2,1)S(1)} collective-permute-done((bf16[2,2,128,128]{3,2,1,0:T(8,128)(2,1)S(1)}, bf16[2,2,128,128]{3,2,1,0:T(8,128)(2,1)S(1)}, u32[]{:S(2)}, u32[]{:S(2)}) %collective-permute-start.32) | collective-permute-done | bytes 131104 | tf_op jit(solution)/shard_map/ppermute | solution.py:69
  109.6 0.2 collective-permute-start.25
  109.8 0.1 collective-permute-start.26
  109.9 1.3 %collective-permute-done.28.refs_1_ = bf16[2,2,128,128]{3,2,1,0:T(8,128)(2,1)S(1)} collective-permute-done((bf16[2,2,128,128]{3,2,1,0:T(8,128)(2,1)S(1)}, bf16[2,2,128,128]{3,2,1,0:T(8,128)(2,1)S(1)}, u32[]{:S(2)}, u32[]{:S(2)}) %collective-permute-start.28) | collective-permute-done | bytes 131104 | tf_op jit(solution)/shard_map/ppermute | solution.py:69
  111.3 1.9 %collective-permute-start.27 = (bf16[1,4,128,128]{3,2,1,0:T(8,128)(2,1)S(1)}, bf16[1,4,128,128]{3,2,1,0:T(8,128)(2,1)S(1)}, u32[]{:S(2)}, u32[]{:S(2)}) collective-permute-start(bf16[1,4,128,128]{3,2,1,0:T(8,128)(2,1)S(1)} %get-tuple-element.58), channel_id=1, source_target_pairs={{0,6},{1,7},{2,4},{3,5},{4,2},{5,3},{6,0},{7,1},{8,14},{9,15},{10,... | collective-permute-start | bytes 393224 | tf_op jit(solution)/shard_map/ppermute | solution.py:69
  113.1 2.1 %collective-permute-done.29.refs_2_ = bf16[2,2,128,128]{3,2,1,0:T(8,128)(2,1)S(1)} collective-permute-done((bf16[2,2,128,128]{3,2,1,0:T(8,128)(2,1)S(1)}, bf16[2,2,128,128]{3,2,1,0:T(8,128)(2,1)S(1)}, u32[]{:S(2)}, u32[]{:S(2)}) %collective-permute-start.29) | collective-permute-done | bytes 131104 | tf_op jit(solution)/shard_map/ppermute | solution.py:69
  115.3 1.7 %shard_map.99 = (bf16[512,512]{1,0:T(8,128)(2,1)}, bf16[512,512]{1,0:T(8,128)(2,1)}) custom-call(s32[3]{0:T(128)S(1)} %pad_add_fusion.ids, bf16[2,2,128,128]{3,2,1,0:T(8,128)(2,1)S(1)} %get-tuple-element.59.refs_0_, bf16[2,2,128,128]{3,2,1,0:T(8,128)(2,1)S(1)} %collective-permute-done.28.refs_1_, ...), custom_call_target="tpu_custom_call" | custom-call | bytes 5250000 | tf_op jit(solution)/shard_map/pallas_call | solution.py:477
  117.0 3.2 %collective-permute-done.26.refs_2_ = bf16[1,4,128,128]{3,2,1,0:T(8,128)(2,1)S(1)} collective-permute-done((bf16[1,4,128,128]{3,2,1,0:T(8,128)(2,1)S(1)}, bf16[1,4,128,128]{3,2,1,0:T(8,128)(2,1)S(1)}, u32[]{:S(2)}, u32[]{:S(2)}) %collective-permute-start.26) | collective-permute-done | bytes 131104 | tf_op jit(solution)/shard_map/ppermute | solution.py:69
  120.2 1.4 %shard_map.98 = bf16[512,512]{1,0:T(8,128)(2,1)} custom-call(s32[3]{0:T(128)S(1)} %pad_add_fusion.ids, bf16[1,4,128,128]{3,2,1,0:T(8,128)(2,1)S(1)} %get-tuple-element.55.refs_0_, bf16[1,4,128,128]{3,2,1,0:T(8,128)(2,1)S(1)} %collective-permute-done.25.refs_1_, bf16[1,4,128,128]{3,2,1,0:T(8,128)(2,1)S(1)} %collective-permute-done.26.refs_2_, ...), custom_call_target="tpu_custom_call" | custom-call | bytes 5250000 | tf_op jit(solution)/shard_map/pallas_call | solution.py:477
  (94 shorter events, 1.1 us)
Async XLA Ops:
  0.7 1.0 copy-start
  1.8 11.6 %copy-start.2 = (bf16[128,2048]{1,0:T(8,128)(2,1)S(1)}, bf16[128,2048]{1,0:T(8,128)(2,1)}, u32[]{:S(2)}) copy-start(bf16[128,2048]{1,0:T(8,128)(2,1)} %g_ref.1) | copy-start | bytes 1572868
  2.6 18.6 %collective-permute-start = (bf16[4,128,128]{2,1,0:T(8,128)(2,1)S(1)}, bf16[4,128,128]{2,1,0:T(8,128)(2,1)S(1)}, u32[]{:S(2)}, u32[]{:S(2)}) collective-permute-start(bf16[4,128,128]{2,1,0:T(8,128)(2,1)S(1)} %get-tuple-element.39), channel_id=1, source_target_pairs={{0,8},{8,0},{16,24},{24,16},{1,9},{9,1},{17,25},{25,17},{2,10},{10... | collective-permute-start | bytes 393224 | tf_op jit(solution)/shard_map/ppermute | solution.py:64
  5.7 23.1 %collective-permute-start.1 = (bf16[4,128,128]{2,1,0:T(8,128)(2,1)S(1)}, bf16[4,128,128]{2,1,0:T(8,128)(2,1)S(1)}, u32[]{:S(2)}, u32[]{:S(2)}) collective-permute-start(bf16[4,128,128]{2,1,0:T(8,128)(2,1)S(1)} %get-tuple-element.40), channel_id=1, source_target_pairs={{0,16},{8,24},{16,0},{24,8},{1,17},{9,25},{17,1},{25,9},{2,18},{10... | collective-permute-start | bytes 393224 | tf_op jit(solution)/shard_map/ppermute | solution.py:64
  8.3 21.5 %collective-permute-start.2 = (bf16[4,128,128]{2,1,0:T(8,128)(2,1)S(1)}, bf16[4,128,128]{2,1,0:T(8,128)(2,1)S(1)}, u32[]{:S(2)}, u32[]{:S(2)}) collective-permute-start(bf16[4,128,128]{2,1,0:T(8,128)(2,1)S(1)} %get-tuple-element.41), channel_id=1, source_target_pairs={{0,24},{8,16},{16,8},{24,0},{1,25},{9,17},{17,9},{25,1},{2,26},{10... | collective-permute-start | bytes 393224 | tf_op jit(solution)/shard_map/ppermute | solution.py:64
  8.3 1.0 copy-start.1
  10.1 11.4 %collective-permute-start.14 = (bf16[4,128,128]{2,1,0:T(8,128)(2,1)S(1)}, bf16[4,128,128]{2,1,0:T(8,128)(2,1)S(1)}, u32[]{:S(2)}, u32[]{:S(2)}) collective-permute-start(bf16[4,128,128]{2,1,0:T(8,128)(2,1)S(1)} %get-tuple-element.47), channel_id=1, source_target_pairs={{0,2},{1,3},{2,0},{3,1},{4,6},{5,7},{6,4},{7,5},{8,10},{9,11},{10,... | collective-permute-start | bytes 393224 | tf_op jit(solution)/shard_map/ppermute | solution.py:69
  11.9 11.4 %collective-permute-start.15 = (bf16[4,128,128]{2,1,0:T(8,128)(2,1)S(1)}, bf16[4,128,128]{2,1,0:T(8,128)(2,1)S(1)}, u32[]{:S(2)}, u32[]{:S(2)}) collective-permute-start(bf16[4,128,128]{2,1,0:T(8,128)(2,1)S(1)} %get-tuple-element.48), channel_id=1, source_target_pairs={{0,4},{1,5},{2,6},{3,7},{4,0},{5,1},{6,2},{7,3},{8,12},{9,13},{10,... | collective-permute-start | bytes 393224 | tf_op jit(solution)/shard_map/ppermute | solution.py:69
  13.4 1.0 copy-start.3
  14.4 1.0 copy-start.4
  15.5 2.2 %copy-start.5 = (s32[8,4,4]{0,2,1:T(4,128)S(1)}, s32[8,4,4]{0,2,1:T(4,128)}, u32[]{:S(2)}) copy-start(s32[8,4,4]{0,2,1:T(4,128)} %param.13) | copy-start | bytes 1540
  15.5 2.2 %copy-start.6 = (s32[8]{0:T(128)S(1)}, s32[8]{0:T(128)}, u32[]{:S(2)}) copy-start(s32[8]{0:T(128)} %order.1) | copy-start | bytes 100
  21.2 7.3 %collective-permute-start.16 = (bf16[4,128,128]{2,1,0:T(8,128)(2,1)S(1)}, bf16[4,128,128]{2,1,0:T(8,128)(2,1)S(1)}, u32[]{:S(2)}, u32[]{:S(2)}) collective-permute-start(bf16[4,128,128]{2,1,0:T(8,128)(2,1)S(1)} %get-tuple-element.49), channel_id=1, source_target_pairs={{0,6},{1,7},{2,4},{3,5},{4,2},{5,3},{6,0},{7,1},{8,14},{9,15},{10,... | collective-permute-start | bytes 393224 | tf_op jit(solution)/shard_map/ppermute | solution.py:69
  21.5 30.9 %collective-permute-start.7 = (bf16[4,264,128]{2,1,0:T(8,128)(2,1)S(1)}, bf16[4,264,128]{2,1,0:T(8,128)(2,1)S(1)}, u32[]{:S(2)}, u32[]{:S(2)}) collective-permute-start(bf16[4,264,128]{2,1,0:T(8,128)(2,1)S(1)} %get-tuple-element.43), channel_id=1, source_target_pairs={{0,2},{1,3},{2,0},{3,1},{4,6},{5,7},{6,4},{7,5},{8,10},{9,11},{10,... | collective-permute-start | bytes 811016 | tf_op jit(solution)/shard_map/ppermute | solution.py:69
  23.3 29.1 %collective-permute-start.8 = (bf16[4,264,128]{2,1,0:T(8,128)(2,1)S(1)}, bf16[4,264,128]{2,1,0:T(8,128)(2,1)S(1)}, u32[]{:S(2)}, u32[]{:S(2)}) collective-permute-start(bf16[4,264,128]{2,1,0:T(8,128)(2,1)S(1)} %get-tuple-element.44), channel_id=1, source_target_pairs={{0,4},{1,5},{2,6},{3,7},{4,0},{5,1},{6,2},{7,3},{8,12},{9,13},{10,... | collective-permute-start | bytes 811016 | tf_op jit(solution)/shard_map/ppermute | solution.py:69
  28.5 23.9 %collective-permute-start.9 = (bf16[4,264,128]{2,1,0:T(8,128)(2,1)S(1)}, bf16[4,264,128]{2,1,0:T(8,128)(2,1)S(1)}, u32[]{:S(2)}, u32[]{:S(2)}) collective-permute-start(bf16[4,264,128]{2,1,0:T(8,128)(2,1)S(1)} %get-tuple-element.45), channel_id=1, source_target_pairs={{0,6},{1,7},{2,4},{3,5},{4,2},{5,3},{6,0},{7,1},{8,14},{9,15},{10,... | collective-permute-start | bytes 811016 | tf_op jit(solution)/shard_map/ppermute | solution.py:69
  28.8 5.0 %collective-permute-start.17 = (bf16[4,128,128]{2,1,0:T(8,128)(2,1)S(1)}, bf16[4,128,128]{2,1,0:T(8,128)(2,1)S(1)}, u32[]{:S(2)}, u32[]{:S(2)}) collective-permute-start(bf16[4,128,128]{2,1,0:T(8,128)(2,1)S(1)} %pad_maximum_fusion.6), channel_id=1, source_target_pairs={{0,8},{8,0},{16,24},{24,16},{1,9},{9,1},{17,25},{25,17},{2,10},{10... | collective-permute-start | bytes 393224 | tf_op jit(solution)/shard_map/ppermute | solution.py:64
  29.9 9.6 %collective-permute-start.3 = (bf16[4,128,128]{2,1,0:T(8,128)(2,1)S(1)}, bf16[4,128,128]{2,1,0:T(8,128)(2,1)S(1)}, u32[]{:S(2)}, u32[]{:S(2)}) collective-permute-start(bf16[4,128,128]{2,1,0:T(8,128)(2,1)S(1)} %pad_maximum_fusion.3), channel_id=1, source_target_pairs={{0,2},{1,3},{2,0},{3,1},{4,6},{5,7},{6,4},{7,5},{8,10},{9,11},{10,... | collective-permute-start | bytes 393224 | tf_op jit(solution)/shard_map/ppermute | solution.py:69
  33.9 7.2 %collective-permute-start.4 = (bf16[4,128,128]{2,1,0:T(8,128)(2,1)S(1)}, bf16[4,128,128]{2,1,0:T(8,128)(2,1)S(1)}, u32[]{:S(2)}, u32[]{:S(2)}) collective-permute-start(bf16[4,128,128]{2,1,0:T(8,128)(2,1)S(1)} %pad_maximum_fusion.4), channel_id=1, source_target_pairs={{0,4},{1,5},{2,6},{3,7},{4,0},{5,1},{6,2},{7,3},{8,12},{9,13},{10,... | collective-permute-start | bytes 393224 | tf_op jit(solution)/shard_map/ppermute | solution.py:69
  39.5 5.9 %collective-permute-start.5 = (bf16[4,128,128]{2,1,0:T(8,128)(2,1)S(1)}, bf16[4,128,128]{2,1,0:T(8,128)(2,1)S(1)}, u32[]{:S(2)}, u32[]{:S(2)}) collective-permute-start(bf16[4,128,128]{2,1,0:T(8,128)(2,1)S(1)} %pad_maximum_fusion.5), channel_id=1, source_target_pairs={{0,6},{1,7},{2,4},{3,5},{4,2},{5,3},{6,0},{7,1},{8,14},{9,15},{10,... | collective-permute-start | bytes 393224 | tf_op jit(solution)/shard_map/ppermute | solution.py:69
  41.0 9.3 %collective-permute-start.18 = (bf16[4,128,128]{2,1,0:T(8,128)(2,1)S(1)}, bf16[4,128,128]{2,1,0:T(8,128)(2,1)S(1)}, u32[]{:S(2)}, u32[]{:S(2)}) collective-permute-start(bf16[4,128,128]{2,1,0:T(8,128)(2,1)S(1)} %pad_maximum_fusion.7), channel_id=1, source_target_pairs={{0,16},{8,24},{16,0},{24,8},{1,17},{9,25},{17,1},{25,9},{2,18},{10... | collective-permute-start | bytes 393224 | tf_op jit(solution)/shard_map/ppermute | solution.py:64
  45.4 6.9 %collective-permute-start.19 = (bf16[4,128,128]{2,1,0:T(8,128)(2,1)S(1)}, bf16[4,128,128]{2,1,0:T(8,128)(2,1)S(1)}, u32[]{:S(2)}, u32[]{:S(2)}) collective-permute-start(bf16[4,128,128]{2,1,0:T(8,128)(2,1)S(1)} %pad_maximum_fusion.8), channel_id=1, source_target_pairs={{0,24},{8,16},{16,8},{24,0},{1,25},{9,17},{17,9},{25,1},{2,26},{10... | collective-permute-start | bytes 393224 | tf_op jit(solution)/shard_map/ppermute | solution.py:64
  50.4 20.2 %collective-permute-start.6 = (bf16[16,128,128]{2,1,0:T(8,128)(2,1)S(1)}, bf16[16,128,128]{2,1,0:T(8,128)(2,1)S(1)}, u32[]{:S(2)}, u32[]{:S(2)}) collective-permute-start(bf16[16,128,128]{2,1,0:T(8,128)(2,1)S(1)} %get-tuple-element.142), channel_id=1, source_target_pairs={{0,1},{1,0},{2,3},{3,2},{4,5},{5,4},{6,7},{7,6},{8,9},{9,8},{10,11... | collective-permute-start | bytes 1572872 | tf_op jit(solution)/shard_map/ppermute | solution.py:69
  52.5 5.9 %collective-permute-start.10 = (bf16[4,136,128]{2,1,0:T(8,128)(2,1)S(1)}, bf16[4,136,128]{2,1,0:T(8,128)(2,1)S(1)}, u32[]{:S(2)}, u32[]{:S(2)}) collective-permute-start(bf16[4,136,128]{2,1,0:T(8,128)(2,1)S(1)} %pad_maximum_fusion), channel_id=1, source_target_pairs={{0,8},{8,0},{16,24},{24,16},{1,9},{9,1},{17,25},{25,17},{2,10},{10... | collective-permute-start | bytes 417800 | tf_op jit(solution)/shard_map/ppermute | solution.py:64
  54.2 11.3 %collective-permute-start.11 = (bf16[4,136,128]{2,1,0:T(8,128)(2,1)S(1)}, bf16[4,136,128]{2,1,0:T(8,128)(2,1)S(1)}, u32[]{:S(2)}, u32[]{:S(2)}) collective-permute-start(bf16[4,136,128]{2,1,0:T(8,128)(2,1)S(1)} %pad_maximum_fusion.1), channel_id=1, source_target_pairs={{0,16},{8,24},{16,0},{24,8},{1,17},{9,25},{17,1},{25,9},{2,18},{10... | collective-permute-start | bytes 417800 | tf_op jit(solution)/shard_map/ppermute | solution.py:64
  56.7 8.8 %collective-permute-start.12 = (bf16[4,136,128]{2,1,0:T(8,128)(2,1)S(1)}, bf16[4,136,128]{2,1,0:T(8,128)(2,1)S(1)}, u32[]{:S(2)}, u32[]{:S(2)}) collective-permute-start(bf16[4,136,128]{2,1,0:T(8,128)(2,1)S(1)} %pad_maximum_fusion.2), channel_id=1, source_target_pairs={{0,24},{8,16},{16,8},{24,0},{1,25},{9,17},{17,9},{25,1},{2,26},{10... | collective-permute-start | bytes 417800 | tf_op jit(solution)/shard_map/ppermute | solution.py:64
  65.8 10.8 %collective-permute-start.13 = (bf16[16,136,128]{2,1,0:T(8,128)(2,1)S(1)}, bf16[16,136,128]{2,1,0:T(8,128)(2,1)S(1)}, u32[]{:S(2)}, u32[]{:S(2)}) collective-permute-start(bf16[16,136,128]{2,1,0:T(8,128)(2,1)S(1)} %get-tuple-element.105), channel_id=1, source_target_pairs={{0,1},{1,0},{2,3},{3,2},{4,5},{5,4},{6,7},{7,6},{8,9},{9,8},{10,11... | collective-permute-start | bytes 1671176 | tf_op jit(solution)/shard_map/ppermute | solution.py:69
  65.9 23.0 %collective-permute-start.21 = (bf16[4,128,128]{2,1,0:T(8,128)(2,1)S(1)}, bf16[4,128,128]{2,1,0:T(8,128)(2,1)S(1)}, u32[]{:S(2)}, u32[]{:S(2)}) collective-permute-start(bf16[4,128,128]{2,1,0:T(8,128)(2,1)S(1)} %pad_maximum_fusion.9), channel_id=1, source_target_pairs={{0,16},{8,24},{16,0},{24,8},{1,17},{9,25},{17,1},{25,9},{2,18},{10... | collective-permute-start | bytes 393224 | tf_op jit(solution)/shard_map/ppermute | solution.py:64
  68.9 20.0 %collective-permute-start.22 = (bf16[4,128,128]{2,1,0:T(8,128)(2,1)S(1)}, bf16[4,128,128]{2,1,0:T(8,128)(2,1)S(1)}, u32[]{:S(2)}, u32[]{:S(2)}) collective-permute-start(bf16[4,128,128]{2,1,0:T(8,128)(2,1)S(1)} %pad_maximum_fusion.10), channel_id=1, source_target_pairs={{0,24},{8,16},{16,8},{24,0},{1,25},{9,17},{17,9},{25,1},{2,26},{10... | collective-permute-start | bytes 393224 | tf_op jit(solution)/shard_map/ppermute | solution.py:64
  70.4 9.7 %collective-permute-start.23 = (bf16[4,128,128]{2,1,0:T(8,128)(2,1)S(1)}, bf16[4,128,128]{2,1,0:T(8,128)(2,1)S(1)}, u32[]{:S(2)}, u32[]{:S(2)}) collective-permute-start(bf16[4,128,128]{2,1,0:T(8,128)(2,1)S(1)} %pad_maximum_fusion.12), channel_id=1, source_target_pairs={{0,8},{8,0},{16,24},{24,16},{1,9},{9,1},{17,25},{25,17},{2,10},{10... | collective-permute-start | bytes 393224 | tf_op jit(solution)/shard_map/ppermute | solution.py:64
  76.4 1.2 %collective-permute-start.20 = (f32[32,128]{1,0:T(8,128)S(1)}, f32[32,128]{1,0:T(8,128)S(1)}, u32[]{:S(2)}, u32[]{:S(2)}) collective-permute-start(f32[32,128]{1,0:T(8,128)S(1)} %totals.1.refs_0_), channel_id=1, source_target_pairs={{0,1},{1,0},{2,3},{3,2},{4,5},{5,4},{6,7},{7,6},{8,9},{9,8},{10,11... | collective-permute-start | bytes 49160 | tf_op jit(solution)/shard_map/ppermute | solution.py:69
  98.0 6.1 %collective-permute-start.24 = (f32[16,128,128]{2,1,0:T(8,128)S(1)}, f32[16,128,128]{2,1,0:T(8,128)S(1)}, u32[]{:S(2)}, u32[]{:S(2)}) collective-permute-start(f32[16,128,128]{2,1,0:T(8,128)S(1)} %get-tuple-element.54), channel_id=1, source_target_pairs={{0,1},{1,0},{2,3},{3,2},{4,5},{5,4},{6,7},{7,6},{8,9},{9,8},{10,11... | collective-permute-start | bytes 3145736 | tf_op jit(solution)/shard_map/ppermute | solution.py:69
  98.1 6.7 %collective-permute-start.31 = (bf16[2,2,128,128]{3,2,1,0:T(8,128)(2,1)S(1)}, bf16[2,2,128,128]{3,2,1,0:T(8,128)(2,1)S(1)}, u32[]{:S(2)}, u32[]{:S(2)}) collective-permute-start(bf16[2,2,128,128]{3,2,1,0:T(8,128)(2,1)S(1)} %get-tuple-element.64), channel_id=1, source_target_pairs={{0,2},{1,3},{2,0},{3,1},{4,6},{5,7},{6,4},{7,5},{8,10},{9,11},{10,... | collective-permute-start | bytes 393224 | tf_op jit(solution)/shard_map/ppermute | solution.py:69
  100.6 9.1 %collective-permute-start.32 = (bf16[2,2,128,128]{3,2,1,0:T(8,128)(2,1)S(1)}, bf16[2,2,128,128]{3,2,1,0:T(8,128)(2,1)S(1)}, u32[]{:S(2)}, u32[]{:S(2)}) collective-permute-start(bf16[2,2,128,128]{3,2,1,0:T(8,128)(2,1)S(1)} %get-tuple-element.65), channel_id=1, source_target_pairs={{0,4},{1,5},{2,6},{3,7},{4,0},{5,1},{6,2},{7,3},{8,12},{9,13},{10,... | collective-permute-start | bytes 393224 | tf_op jit(solution)/shard_map/ppermute | solution.py:69
  100.6 9.3 %collective-permute-start.33 = (bf16[2,2,128,128]{3,2,1,0:T(8,128)(2,1)S(1)}, bf16[2,2,128,128]{3,2,1,0:T(8,128)(2,1)S(1)}, u32[]{:S(2)}, u32[]{:S(2)}) collective-permute-start(bf16[2,2,128,128]{3,2,1,0:T(8,128)(2,1)S(1)} %get-tuple-element.66), channel_id=1, source_target_pairs={{0,6},{1,7},{2,4},{3,5},{4,2},{5,3},{6,0},{7,1},{8,14},{9,15},{10,... | collective-permute-start | bytes 393224 | tf_op jit(solution)/shard_map/ppermute | solution.py:69
  102.1 9.1 %collective-permute-start.28 = (bf16[2,2,128,128]{3,2,1,0:T(8,128)(2,1)S(1)}, bf16[2,2,128,128]{3,2,1,0:T(8,128)(2,1)S(1)}, u32[]{:S(2)}, u32[]{:S(2)}) collective-permute-start(bf16[2,2,128,128]{3,2,1,0:T(8,128)(2,1)S(1)} %get-tuple-element.60), channel_id=1, source_target_pairs={{0,2},{1,3},{2,0},{3,1},{4,6},{5,7},{6,4},{7,5},{8,10},{9,11},{10,... | collective-permute-start | bytes 393224 | tf_op jit(solution)/shard_map/ppermute | solution.py:69
  104.1 11.2 %collective-permute-start.29 = (bf16[2,2,128,128]{3,2,1,0:T(8,128)(2,1)S(1)}, bf16[2,2,128,128]{3,2,1,0:T(8,128)(2,1)S(1)}, u32[]{:S(2)}, u32[]{:S(2)}) collective-permute-start(bf16[2,2,128,128]{3,2,1,0:T(8,128)(2,1)S(1)} %get-tuple-element.61), channel_id=1, source_target_pairs={{0,4},{1,5},{2,6},{3,7},{4,0},{5,1},{6,2},{7,3},{8,12},{9,13},{10,... | collective-permute-start | bytes 393224 | tf_op jit(solution)/shard_map/ppermute | solution.py:69
  104.8 10.4 %collective-permute-start.30 = (bf16[2,2,128,128]{3,2,1,0:T(8,128)(2,1)S(1)}, bf16[2,2,128,128]{3,2,1,0:T(8,128)(2,1)S(1)}, u32[]{:S(2)}, u32[]{:S(2)}) collective-permute-start(bf16[2,2,128,128]{3,2,1,0:T(8,128)(2,1)S(1)} %get-tuple-element.62), channel_id=1, source_target_pairs={{0,6},{1,7},{2,4},{3,5},{4,2},{5,3},{6,0},{7,1},{8,14},{9,15},{10,... | collective-permute-start | bytes 393224 | tf_op jit(solution)/shard_map/ppermute | solution.py:69
  109.6 7.3 %collective-permute-start.25 = (bf16[1,4,128,128]{3,2,1,0:T(8,128)(2,1)S(1)}, bf16[1,4,128,128]{3,2,1,0:T(8,128)(2,1)S(1)}, u32[]{:S(2)}, u32[]{:S(2)}) collective-permute-start(bf16[1,4,128,128]{3,2,1,0:T(8,128)(2,1)S(1)} %get-tuple-element.56), channel_id=1, source_target_pairs={{0,2},{1,3},{2,0},{3,1},{4,6},{5,7},{6,4},{7,5},{8,10},{9,11},{10,... | collective-permute-start | bytes 393224 | tf_op jit(solution)/shard_map/ppermute | solution.py:69
  109.8 10.3 %collective-permute-start.26 = (bf16[1,4,128,128]{3,2,1,0:T(8,128)(2,1)S(1)}, bf16[1,4,128,128]{3,2,1,0:T(8,128)(2,1)S(1)}, u32[]{:S(2)}, u32[]{:S(2)}) collective-permute-start(bf16[1,4,128,128]{3,2,1,0:T(8,128)(2,1)S(1)} %get-tuple-element.57), channel_id=1, source_target_pairs={{0,4},{1,5},{2,6},{3,7},{4,0},{5,1},{6,2},{7,3},{8,12},{9,13},{10,... | collective-permute-start | bytes 393224 | tf_op jit(solution)/shard_map/ppermute | solution.py:69
  111.3 8.9 %collective-permute-start.27 = (bf16[1,4,128,128]{3,2,1,0:T(8,128)(2,1)S(1)}, bf16[1,4,128,128]{3,2,1,0:T(8,128)(2,1)S(1)}, u32[]{:S(2)}, u32[]{:S(2)}) collective-permute-start(bf16[1,4,128,128]{3,2,1,0:T(8,128)(2,1)S(1)} %get-tuple-element.58), channel_id=1, source_target_pairs={{0,6},{1,7},{2,4},{3,5},{4,2},{5,3},{6,0},{7,1},{8,14},{9,15},{10,... | collective-permute-start | bytes 393224 | tf_op jit(solution)/shard_map/ppermute | solution.py:69
where the time goes:
time: 122 us
  starting transfers between devices  42.5 us (35%)
  waiting for transfers between devices  38.2 us (31%)
  Pallas kernels  34.3 us (28%)
  local copies, waits for them, and re-layouts  5.1 us (4%)
    ppermute x22, waiting for transfers between devices, over_frame(): return lax.ppermute(value, 'frame', [(i, i ^ step) for i in range(count)])  22.2 us
    ppermute x22, starting transfers between devices, over_frame(): return lax.ppermute(value, 'frame', [(i, i ^ step) for i in range(count)])  21.4 us
    ppermute x12, starting transfers between devices, over_head(): return lax.ppermute(value, 'head', [(i, i ^ step) for i in range(count)])  21.1 us
    pallas_call x2, Pallas kernels, grads(): pl.pallas_call(functools.partial(grads_kernel, plan, span, first, last),...  17.8 us
    ppermute x12, waiting for transfers between devices, over_head(): return lax.ppermute(value, 'head', [(i, i ^ step) for i in range(count)])  16 us
    pallas_call x1, Pallas kernels, totals(): pl.pallas_call(functools.partial(totals_kernel, plan), out_shape=sds((pla...  5.8 us
    unnamed x49, local copies, waits for them, and re-layouts  4.75 us
    pallas_call x1, Pallas kernels, lists(): pl.pallas_call(functools.partial(lists_kernel, plan), out_shape=[sds((own...  3.48 us
  transfers between devices with their start and end apart: 34, of which 15 were waited for; matrix products, arithmetic and copies ran while one was open for 1% of the time, Pallas kernels for 19%

commit v1 on v0

--- a/solution.py
+++ b/solution.py
@@ -85,32 +85,45 @@
     return pl.ds(pl.multiple_of((ids[1] ^ s) * HEAD_DIM, HEAD_DIM), HEAD_DIM)
 
 
-def prep_kernel(plan, head_first, ids, x_ref, *refs):
-    outs, buf, sems = refs[:-2], refs[-2], refs[-1]
-    copies = bundles(plan, ids, [x_ref], [buf], sems)
-    for r in range(plan.nz):
-        copies[r].wait()
-        for s in range(plan.na):
-            piece = buf[r, :, within_bundle(ids, s)]
-            if head_first:
-                outs[r][s] = piece
-            else:
-                outs[s][r] = piece
-
-
-def prep(plan, ids, x, head_first):
-    pieces, chunk = (plan.nz, plan.na) if head_first else (plan.na, plan.nz)
-    return pl.pallas_call(
-        functools.partial(prep_kernel, plan, head_first),
-        out_shape=[sds((chunk, plan.rows, HEAD_DIM), BF16)] * pieces,
-        in_specs=[SMEM, HBM],
-        out_specs=[VMEM] * pieces,
-        scratch_shapes=[
-            pltpu.VMEM((plan.nz, plan.rows, plan.hh * HEAD_DIM), BF16),
-            pltpu.SemaphoreType.DMA((1, plan.nz)),
-        ],
-        cost_estimate=lasts(1.2),
+def prep_kernel(plan, q_ref, k_ref, out):
+    hd, rows = HEAD_DIM, plan.rows
+    for a in range(plan.na):
+        for z in range(plan.nz):
+            head, place = z * plan.hh + a, a * plan.nz + z
+            out[place, :rows] = q_ref[:, head * hd : (head + 1) * hd]
+            out[place, rows:] = k_ref[:, head * hd : (head + 1) * hd]
+
+
+def prep(plan, q, k):
+    return pl.pallas_call(
+        functools.partial(prep_kernel, plan),
+        out_shape=sds((plan.own, 2 * plan.rows, HEAD_DIM), BF16),
+        in_specs=[VMEM] * 2,
+        out_specs=VMEM,
+        cost_estimate=lasts(1.5),
+        compiler_params=within(q, k, q, k),
+        name="prep",
+    )(q, k)
+
+
+def part_kernel(plan, ids, x_ref, q_out, k_out):
+    rows = plan.rows
+    for s in range(plan.na):
+        for r in range(plan.nz):
+            place = (ids[1] ^ s) * plan.nz + (ids[0] ^ r)
+            q_out[s * plan.nz + r] = x_ref[place, :rows]
+            k_out[s * plan.nz + r] = x_ref[place, rows:]
+
+
+def part(plan, ids, x):
+    return pl.pallas_call(
+        functools.partial(part_kernel, plan),
+        out_shape=[sds((plan.own, plan.rows, HEAD_DIM), BF16)] * 2,
+        in_specs=[SMEM, VMEM],
+        out_specs=[VMEM] * 2,
+        cost_estimate=lasts(1),
         compiler_params=within(x, x),
+        name="part",
     )(ids, x)
 
 
@@ -508,18 +521,19 @@
     def regroup(pieces):
         return [jnp.concatenate([p[i : i + 1] for p in pieces]) for i in range(pieces[0].shape[0])]
 
-    def flat_frames_first(by_frame):
-        return jnp.concatenate(by_frame)
-
     def flat_heads_first(by_head):
         return jnp.concatenate([p[s : s + 1] for s in range(na) for p in by_head])
 
-    q_sent = head_stage(prep(plan, ids, queries, True))
-    k_near = frame_stage(prep(plan, ids, key_states, False))
+    groups = [
+        [(a * nb + b) * nz + z for a in range(na) for z in range(nz)] for b in range(nb)
+    ]
+    mine = lax.all_to_all(
+        prep(plan, queries, key_states), ("frame", "head"), 0, 0,
+        tiled=True, axis_index_groups=groups,
+    )
     gv_near = frame_stage(prep_rest(plan, ids, grad_out, attn_out, value_states))
     by_key, n_key = lists(plan, ids, frame_order, block_live.transpose(1, 2, 0))
-    keys = flat_heads_first(head_stage(regroup(k_near)))
-    q_own = flat_frames_first(frame_stage(regroup(q_sent)))
+    q_own, keys = part(plan, ids, mine)
     q_all = jnp.concatenate(swapped([q_own] * nb))
     g_own = flat_heads_first(head_stage(regroup([p[:, : plan.rows + EXTRA] for p in gv_near])))
     g_all = jnp.concatenate(swapped([g_own] * nb))

time: 122 us -> 119 us (0.975)
  the two profiles are of different devices: /device:TPU:0 before, /device:TPU:4 now
where the time goes in v1:
time: 119 us; the launch traced here: 117 us
  starting transfers between devices  37.9 us (32%)
  Pallas kernels  34.6 us (29%)
  waiting for transfers between devices  30.6 us (26%)
  local copies, waits for them, and re-layouts  12.3 us (10%)
    ppermute x16, waiting for transfers between devices, over_frame(): return lax.ppermute(value, 'frame', [(i, i ^ step) for i in range(count)])  20.8 us
    pallas_call x2, Pallas kernels, grads(): pl.pallas_call(functools.partial(grads_kernel, plan, span, first, last),...  17.8 us
    ppermute x16, starting transfers between devices, over_frame(): return lax.ppermute(value, 'frame', [(i, i ^ step) for i in range(count)])  16.8 us
    ppermute x6, starting transfers between devices, over_head(): return lax.ppermute(value, 'head', [(i, i ^ step) for i in range(count)])  13.7 us
    unnamed x30, local copies, waits for them, and re-layouts  11.4 us
    ppermute x6, waiting for transfers between devices, over_head(): return lax.ppermute(value, 'head', [(i, i ^ step) for i in range(count)])  9.81 us
    all_to_all x1, starting transfers between devices, local(): lax.all_to_all(prep(plan, queries, key_states), ('frame', 'head'), 0, 0,...  7.41 us
    pallas_call x1, Pallas kernels, totals(): pl.pallas_call(functools.partial(totals_kernel, plan), out_shape=sds((pla...  5.8 us
  transfers between devices with their start and end apart: 23, of which 11 were waited for; matrix products, arithmetic and copies ran while one was open for 9% of the time, Pallas kernels for 20%

profile of v1, /device:TPU:4, one launch (start us, length us, event | category | flops | bytes accessed | tf_op | source)
XLA Modules:
  0.0 116.6 jit_solution(5450238824924225237)
XLA Ops:
  0.6 1.0 copy-done.3
  1.7 1.0 copy-done.4
  2.7 1.2 %prep.1 = bf16[16,256,128]{2,1,0:T(8,128)(2,1)} custom-call(bf16[128,2048]{1,0:T(8,128)(2,1)S(1)} %copy-done.3, bf16[128,2048]{1,0:T(8,128)(2,1)S(1)} %copy-done.4), custom_call_target="tpu_custom_call" | custom-call | bytes 5250000 | tf_op jit(solution)/shard_map/prep/pallas_call | solution.py:98
  3.9 7.4 %all-to-all-start = ((bf16[16,256,128]{2,1,0:T(8,128)(2,1)}), bf16[16,256,128]{2,1,0:T(8,128)(2,1)S(1)}, u32[]{:S(2)}, u32[]{:S(2)}) async-start(bf16[16,256,128]{2,1,0:T(8,128)(2,1)} %prep.1), calls=%async_computation | async-start | bytes 2097152 | tf_op jit(solution)/shard_map/all_to_all | solution.py:530
  11.4 0.1 pad_add_fusion.ids
  11.5 2.1 %prep_rest.1 = (bf16[4,264,128]{2,1,0:T(8,128)(2,1)S(1)}, bf16[4,264,128]{2,1,0:T(8,128)(2,1)S(1)}, bf16[4,264,128]{2,1,0:T(8,128)(2,1)S(1)}, bf16[4,264,128]{2,1,0:T(8,128)(2,1)S(1)}) custom-call(s32[3]{0:T(128)S(1)} %pad_add_fusion.ids, bf16[128,2048]{1,0:T(8,128)(2,1)S(1)} %copy-done, bf16[128,2048]{1,0:T(8,128)(2,1)S(1)} %copy-done.1, ...), custom_call_target="tpu_custom_call" | custom-call | bytes 7000000 | tf_op jit(solution)/shard_map/prep_rest/pallas_call | solution.py:157
  13.6 1.5 %collective-permute-start.1 = (bf16[4,264,128]{2,1,0:T(8,128)(2,1)S(1)}, bf16[4,264,128]{2,1,0:T(8,128)(2,1)S(1)}, u32[]{:S(2)}, u32[]{:S(2)}) collective-permute-start(bf16[4,264,128]{2,1,0:T(8,128)(2,1)S(1)} %get-tuple-element.34), channel_id=1, source_target_pairs={{0,2},{1,3},{2,0},{3,1},{4,6},{5,7},{6,4},{7,5},{8,10},{9,11},{10,... | collective-permute-start | bytes 811016 | tf_op jit(solution)/shard_map/ppermute | solution.py:69
  15.1 0.6 collective-permute-start.2
  15.6 1.5 %collective-permute-start.3 = (bf16[4,264,128]{2,1,0:T(8,128)(2,1)S(1)}, bf16[4,264,128]{2,1,0:T(8,128)(2,1)S(1)}, u32[]{:S(2)}, u32[]{:S(2)}) collective-permute-start(bf16[4,264,128]{2,1,0:T(8,128)(2,1)S(1)} %get-tuple-element.36), channel_id=1, source_target_pairs={{0,6},{1,7},{2,4},{3,5},{4,2},{5,3},{6,0},{7,1},{8,14},{9,15},{10,... | collective-permute-start | bytes 811016 | tf_op jit(solution)/shard_map/ppermute | solution.py:69
  17.1 0.6 constant_dynamic-update-slice_fusion.17
  17.8 3.5 %lists.1 = (s32[16,42]{1,0:T(8,128)S(1)}, s32[16]{0:T(128)S(1)}) custom-call(s32[3]{0:T(128)S(1)} %pad_add_fusion.ids, s32[8]{0:T(128)S(1)} %copy-done.6, s32[4,4,8]{2,1,0:T(4,128)S(1)} %bitcast.4), custom_call_target="tpu_custom_call" | custom-call | bytes 10500000 | tf_op jit(solution)/shard_map/lists/pallas_call | solution.py:215
  21.3 8.5 %collective-permute-done.1 = bf16[4,264,128]{2,1,0:T(8,128)(2,1)S(1)} collective-permute-done((bf16[4,264,128]{2,1,0:T(8,128)(2,1)S(1)}, bf16[4,264,128]{2,1,0:T(8,128)(2,1)S(1)}, u32[]{:S(2)}, u32[]{:S(2)}) %collective-permute-start.1) | collective-permute-done | bytes 270368 | tf_op jit(solution)/shard_map/ppermute | solution.py:69
  29.8 4.7 %collective-permute-done.3 = bf16[4,264,128]{2,1,0:T(8,128)(2,1)S(1)} collective-permute-done((bf16[4,264,128]{2,1,0:T(8,128)(2,1)S(1)}, bf16[4,264,128]{2,1,0:T(8,128)(2,1)S(1)}, u32[]{:S(2)}, u32[]{:S(2)}) %collective-permute-start.3) | collective-permute-done | bytes 270368 | tf_op jit(solution)/shard_map/ppermute | solution.py:69
  34.6 5.0 %collective-permute-start.9 = (bf16[4,128,128]{2,1,0:T(8,128)(2,1)S(1)}, bf16[4,128,128]{2,1,0:T(8,128)(2,1)S(1)}, u32[]{:S(2)}, u32[]{:S(2)}) collective-permute-start(bf16[4,128,128]{2,1,0:T(8,128)(2,1)S(1)} %pad_maximum_fusion.3), channel_id=1, source_target_pairs={{0,16},{8,24},{16,0},{24,8},{1,17},{9,25},{17,1},{25,9},{2,18},{10... | collective-permute-start | bytes 393224 | tf_op jit(solution)/shard_map/ppermute | solution.py:64
  39.7 0.4 collective-permute-start.4
  40.1 0.6 collective-permute-start.5
  40.7 3.6 %collective-permute-start.6 = (bf16[4,136,128]{2,1,0:T(8,128)(2,1)S(1)}, bf16[4,136,128]{2,1,0:T(8,128)(2,1)S(1)}, u32[]{:S(2)}, u32[]{:S(2)}) collective-permute-start(bf16[4,136,128]{2,1,0:T(8,128)(2,1)S(1)} %pad_maximum_fusion.2), channel_id=1, source_target_pairs={{0,24},{8,16},{16,8},{24,0},{1,25},{9,17},{17,9},{25,1},{2,26},{10... | collective-permute-start | bytes 417800 | tf_op jit(solution)/shard_map/ppermute | solution.py:64
  44.3 3.2 %collective-permute-done.4 = bf16[4,136,128]{2,1,0:T(8,128)(2,1)S(1)} collective-permute-done((bf16[4,136,128]{2,1,0:T(8,128)(2,1)S(1)}, bf16[4,136,128]{2,1,0:T(8,128)(2,1)S(1)}, u32[]{:S(2)}, u32[]{:S(2)}) %collective-permute-start.4) | collective-permute-done | bytes 139296 | tf_op jit(solution)/shard_map/ppermute | solution.py:64
  47.5 0.6 constant_dynamic-update-slice_fusion.16
  48.2 6.6 %collective-permute-done.5 = bf16[4,136,128]{2,1,0:T(8,128)(2,1)S(1)} collective-permute-done((bf16[4,136,128]{2,1,0:T(8,128)(2,1)S(1)}, bf16[4,136,128]{2,1,0:T(8,128)(2,1)S(1)}, u32[]{:S(2)}, u32[]{:S(2)}) %collective-permute-start.5) | collective-permute-done | bytes 139296 | tf_op jit(solution)/shard_map/ppermute | solution.py:64
  54.7 0.6 constant_dynamic-update-slice_fusion.15
  55.3 0.6 constant_dynamic-update-slice_fusion.14
  56.0 0.6 constant_dynamic-update-slice_fusion.13
  56.6 0.6 constant_dynamic-update-slice_fusion.12
  57.2 0.6 constant_dynamic-update-slice_fusion.11
  57.8 0.6 constant_dynamic-update-slice_fusion.10
  58.4 0.6 constant_dynamic-update-slice_fusion.9
  59.1 0.6 constant_dynamic-update-slice_fusion.8
  59.7 0.6 constant_dynamic-update-slice_fusion.7
  60.3 0.6 constant_dynamic-update-slice_fusion.6
  60.9 0.6 constant_dynamic-update-slice_fusion.5
  61.5 0.6 constant_dynamic-update-slice_fusion.4
  62.2 0.6 constant_dynamic-update-slice_fusion.3
  62.8 0.6 part.1
  63.5 0.6 constant_dynamic-update-slice_fusion.2
  64.1 0.5 collective-permute-start.7
  64.6 3.5 %collective-permute-start.10 = (bf16[4,128,128]{2,1,0:T(8,128)(2,1)S(1)}, bf16[4,128,128]{2,1,0:T(8,128)(2,1)S(1)}, u32[]{:S(2)}, u32[]{:S(2)}) collective-permute-start(bf16[4,128,128]{2,1,0:T(8,128)(2,1)S(1)} %pad_maximum_fusion.4), channel_id=1, source_target_pairs={{0,24},{8,16},{16,8},{24,0},{1,25},{9,17},{17,9},{25,1},{2,26},{10... | collective-permute-start | bytes 393224 | tf_op jit(solution)/shard_map/ppermute | solution.py:64
  68.1 0.7 collective-permute-start.11
  68.9 0.1 constant_dynamic-update-slice_fusion.q_ref
  69.0 5.8 %totals.1.refs_0_ = f32[32,128]{1,0:T(8,128)S(1)} custom-call(s32[16,42]{1,0:T(8,128)S(1)} %get-tuple-element.30.by_key, s32[16]{0:T(128)S(1)} %get-tuple-element.31.n_key, bf16[16,128,128]{2,1,0:T(8,128)(2,1)S(1)} %get-tuple-element.37.k_ref, bf16[32,128,128]{2,1,0:T(8,128)(2,1)S(1)} %constant_dynamic-update-slice_fusion.q_ref), custom_call_target="tpu_custom_call" | custom-call | bytes 21000000 | tf_op jit(solution)/shard_map/totals/pallas_call | solution.py:300
  74.9 0.1 constant_dynamic-update-slice_fusion.18.g_ref
  74.9 1.1 collective-permute-done.8.refs_1_
  76.0 0.3 query_rows.1
  76.3 8.7 %shard_map.94 = (bf16[2,2,128,128]{3,2,1,0:T(8,128)(2,1)S(1)}, bf16[2,2,128,128]{3,2,1,0:T(8,128)(2,1)S(1)}, bf16[2,2,128,128]{3,2,1,0:T(8,128)(2,1)S(1)}, bf16[...) custom-call(s32[16,42]{1,0:T(8,128)S(1)} %get-tuple-element.30.by_key, s32[16]{0:T(128)S(1)} %get-tuple-element.31.n_key, ...), custom_call_target="tpu_custom_call" | custom-call | bytes 24500000 | tf_op jit(solution)/shard_map/pallas_call | solution.py:441
  85.0 9.1 %shard_map.95 = (bf16[2,2,128,128]{3,2,1,0:T(8,128)(2,1)S(1)}, bf16[2,2,128,128]{3,2,1,0:T(8,128)(2,1)S(1)}, bf16[2,2,128,128]{3,2,1,0:T(8,128)(2,1)S(1)}, bf16[...) custom-call(s32[16,42]{1,0:T(8,128)S(1)} %get-tuple-element.30.by_key, ...), custom_call_target="tpu_custom_call" | custom-call | bytes 24500000 | tf_op jit(solution)/shard_map/pallas_call | solution.py:441
  94.2 0.2 collective-permute-start.12
  94.4 0.7 collective-permute-start.19
  95.1 1.4 %collective-permute-start.20 = (bf16[2,2,128,128]{3,2,1,0:T(8,128)(2,1)S(1)}, bf16[2,2,128,128]{3,2,1,0:T(8,128)(2,1)S(1)}, u32[]{:S(2)}, u32[]{:S(2)}) collective-permute-start(bf16[2,2,128,128]{3,2,1,0:T(8,128)(2,1)S(1)} %get-tuple-element.53), channel_id=1, source_target_pairs={{0,4},{1,5},{2,6},{3,7},{4,0},{5,1},{6,2},{7,3},{8,12},{9,13},{10,... | collective-permute-start | bytes 393224 | tf_op jit(solution)/shard_map/ppermute | solution.py:69
  96.5 1.4 %collective-permute-start.21 = (bf16[2,2,128,128]{3,2,1,0:T(8,128)(2,1)S(1)}, bf16[2,2,128,128]{3,2,1,0:T(8,128)(2,1)S(1)}, u32[]{:S(2)}, u32[]{:S(2)}) collective-permute-start(bf16[2,2,128,128]{3,2,1,0:T(8,128)(2,1)S(1)} %get-tuple-element.54), channel_id=1, source_target_pairs={{0,6},{1,7},{2,4},{3,5},{4,2},{5,3},{6,0},{7,1},{8,14},{9,15},{10,... | collective-permute-start | bytes 393224 | tf_op jit(solution)/shard_map/ppermute | solution.py:69
  97.9 0.7 collective-permute-start.16
  98.6 1.4 %collective-permute-start.17 = (bf16[2,2,128,128]{3,2,1,0:T(8,128)(2,1)S(1)}, bf16[2,2,128,128]{3,2,1,0:T(8,128)(2,1)S(1)}, u32[]{:S(2)}, u32[]{:S(2)}) collective-permute-start(bf16[2,2,128,128]{3,2,1,0:T(8,128)(2,1)S(1)} %get-tuple-element.49), channel_id=1, source_target_pairs={{0,4},{1,5},{2,6},{3,7},{4,0},{5,1},{6,2},{7,3},{8,12},{9,13},{10,... | collective-permute-start | bytes 393224 | tf_op jit(solution)/shard_map/ppermute | solution.py:69
  100.0 0.2 pack.1
  100.2 0.6 collective-permute-done.19.refs_5_
  100.8 1.4 %collective-permute-start.18 = (bf16[2,2,128,128]{3,2,1,0:T(8,128)(2,1)S(1)}, bf16[2,2,128,128]{3,2,1,0:T(8,128)(2,1)S(1)}, u32[]{:S(2)}, u32[]{:S(2)}) collective-permute-start(bf16[2,2,128,128]{3,2,1,0:T(8,128)(2,1)S(1)} %get-tuple-element.50), channel_id=1, source_target_pairs={{0,6},{1,7},{2,4},{3,5},{4,2},{5,3},{6,0},{7,1},{8,14},{9,15},{10,... | collective-permute-start | bytes 393224 | tf_op jit(solution)/shard_map/ppermute | solution.py:69
  102.2 0.4 collective-permute-done.20.refs_6_
  102.6 2.5 %collective-permute-start.13 = (bf16[1,4,128,128]{3,2,1,0:T(8,128)(2,1)S(1)}, bf16[1,4,128,128]{3,2,1,0:T(8,128)(2,1)S(1)}, u32[]{:S(2)}, u32[]{:S(2)}) collective-permute-start(bf16[1,4,128,128]{3,2,1,0:T(8,128)(2,1)S(1)} %get-tuple-element.44), channel_id=1, source_target_pairs={{0,2},{1,3},{2,0},{3,1},{4,6},{5,7},{6,4},{7,5},{8,10},{9,11},{10,... | collective-permute-start | bytes 393224 | tf_op jit(solution)/shard_map/ppermute | solution.py:69
  105.1 1.9 %collective-permute-start.14 = (bf16[1,4,128,128]{3,2,1,0:T(8,128)(2,1)S(1)}, bf16[1,4,128,128]{3,2,1,0:T(8,128)(2,1)S(1)}, u32[]{:S(2)}, u32[]{:S(2)}) collective-permute-start(bf16[1,4,128,128]{3,2,1,0:T(8,128)(2,1)S(1)} %get-tuple-element.45), channel_id=1, source_target_pairs={{0,4},{1,5},{2,6},{3,7},{4,0},{5,1},{6,2},{7,3},{8,12},{9,13},{10,... | collective-permute-start | bytes 393224 | tf_op jit(solution)/shard_map/ppermute | solution.py:69
  107.1 0.9 collective-permute-start.15
  108.0 0.2 collective-permute-done.17.refs_2_
  108.2 2.0 %collective-permute-done.18.refs_3_ = bf16[2,2,128,128]{3,2,1,0:T(8,128)(2,1)S(1)} collective-permute-done((bf16[2,2,128,128]{3,2,1,0:T(8,128)(2,1)S(1)}, bf16[2,2,128,128]{3,2,1,0:T(8,128)(2,1)S(1)}, u32[]{:S(2)}, u32[]{:S(2)}) %collective-permute-start.18) | collective-permute-done | bytes 131104 | tf_op jit(solution)/shard_map/ppermute | solution.py:69
  110.2 1.7 %shard_map.97 = (bf16[512,512]{1,0:T(8,128)(2,1)}, bf16[512,512]{1,0:T(8,128)(2,1)}) custom-call(s32[3]{0:T(128)S(1)} %pad_add_fusion.ids, bf16[2,2,128,128]{3,2,1,0:T(8,128)(2,1)S(1)} %get-tuple-element.47.refs_0_, bf16[2,2,128,128]{3,2,1,0:T(8,128)(2,1)S(1)} %collective-permute-done.16.refs_1_, ...), custom_call_target="tpu_custom_call" | custom-call | bytes 5250000 | tf_op jit(solution)/shard_map/pallas_call | solution.py:490
  111.9 0.3 collective-permute-done.13.refs_1_
  112.1 3.1 %collective-permute-done.15.refs_3_ = bf16[1,4,128,128]{3,2,1,0:T(8,128)(2,1)S(1)} collective-permute-done((bf16[1,4,128,128]{3,2,1,0:T(8,128)(2,1)S(1)}, bf16[1,4,128,128]{3,2,1,0:T(8,128)(2,1)S(1)}, u32[]{:S(2)}, u32[]{:S(2)}) %collective-permute-start.15) | collective-permute-done | bytes 131104 | tf_op jit(solution)/shard_map/ppermute | solution.py:69
  115.2 1.4 %shard_map.96 = bf16[512,512]{1,0:T(8,128)(2,1)} custom-call(s32[3]{0:T(128)S(1)} %pad_add_fusion.ids, bf16[1,4,128,128]{3,2,1,0:T(8,128)(2,1)S(1)} %get-tuple-element.43.refs_0_, bf16[1,4,128,128]{3,2,1,0:T(8,128)(2,1)S(1)} %collective-permute-done.13.refs_1_, bf16[1,4,128,128]{3,2,1,0:T(8,128)(2,1)S(1)} %collective-permute-done.14.refs_2_, ...), custom_call_target="tpu_custom_call" | custom-call | bytes 5250000 | tf_op jit(solution)/shard_map/pallas_call | solution.py:490
  (41 shorter events, 0.5 us)
Async XLA Ops:
  0.6 1.0 copy-start.3
  1.7 1.0 copy-start.4
  3.9 7.5 %copy-start = (bf16[128,2048]{1,0:T(8,128)(2,1)S(1)}, bf16[128,2048]{1,0:T(8,128)(2,1)}, u32[]{:S(2)}) copy-start(bf16[128,2048]{1,0:T(8,128)(2,1)} %g_ref.1) | copy-start | bytes 1572868
  3.9 7.5 %copy-start.1 = (bf16[128,2048]{1,0:T(8,128)(2,1)S(1)}, bf16[128,2048]{1,0:T(8,128)(2,1)}, u32[]{:S(2)}) copy-start(bf16[128,2048]{1,0:T(8,128)(2,1)} %o_ref.1) | copy-start | bytes 1572868
  3.9 7.5 %copy-start.2 = (bf16[128,2048]{1,0:T(8,128)(2,1)S(1)}, bf16[128,2048]{1,0:T(8,128)(2,1)}, u32[]{:S(2)}) copy-start(bf16[128,2048]{1,0:T(8,128)(2,1)} %v_ref.1) | copy-start | bytes 1572868
  3.9 58.8 %all-to-all-start = ((bf16[16,256,128]{2,1,0:T(8,128)(2,1)}), bf16[16,256,128]{2,1,0:T(8,128)(2,1)S(1)}, u32[]{:S(2)}, u32[]{:S(2)}) async-start(bf16[16,256,128]{2,1,0:T(8,128)(2,1)} %prep.1), calls=%async_computation | async-start | bytes 2097152 | tf_op jit(solution)/shard_map/all_to_all | solution.py:530
  11.3 6.4 %copy-start.5 = (s32[8,4,4]{0,2,1:T(4,128)S(1)}, s32[8,4,4]{0,2,1:T(4,128)}, u32[]{:S(2)}) copy-start(s32[8,4,4]{0,2,1:T(4,128)} %param.13) | copy-start | bytes 1540
  11.4 6.4 %copy-start.6 = (s32[8]{0:T(128)S(1)}, s32[8]{0:T(128)}, u32[]{:S(2)}) copy-start(s32[8]{0:T(128)} %order.1) | copy-start | bytes 100
  13.6 16.2 %collective-permute-start.1 = (bf16[4,264,128]{2,1,0:T(8,128)(2,1)S(1)}, bf16[4,264,128]{2,1,0:T(8,128)(2,1)S(1)}, u32[]{:S(2)}, u32[]{:S(2)}) collective-permute-start(bf16[4,264,128]{2,1,0:T(8,128)(2,1)S(1)} %get-tuple-element.34), channel_id=1, source_target_pairs={{0,2},{1,3},{2,0},{3,1},{4,6},{5,7},{6,4},{7,5},{8,10},{9,11},{10,... | collective-permute-start | bytes 811016 | tf_op jit(solution)/shard_map/ppermute | solution.py:69
  15.1 14.7 %collective-permute-start.2 = (bf16[4,264,128]{2,1,0:T(8,128)(2,1)S(1)}, bf16[4,264,128]{2,1,0:T(8,128)(2,1)S(1)}, u32[]{:S(2)}, u32[]{:S(2)}) collective-permute-start(bf16[4,264,128]{2,1,0:T(8,128)(2,1)S(1)} %get-tuple-element.35), channel_id=1, source_target_pairs={{0,4},{1,5},{2,6},{3,7},{4,0},{5,1},{6,2},{7,3},{8,12},{9,13},{10,... | collective-permute-start | bytes 811016 | tf_op jit(solution)/shard_map/ppermute | solution.py:69
  15.6 18.9 %collective-permute-start.3 = (bf16[4,264,128]{2,1,0:T(8,128)(2,1)S(1)}, bf16[4,264,128]{2,1,0:T(8,128)(2,1)S(1)}, u32[]{:S(2)}, u32[]{:S(2)}) collective-permute-start(bf16[4,264,128]{2,1,0:T(8,128)(2,1)S(1)} %get-tuple-element.36), channel_id=1, source_target_pairs={{0,6},{1,7},{2,4},{3,5},{4,2},{5,3},{6,0},{7,1},{8,14},{9,15},{10,... | collective-permute-start | bytes 811016 | tf_op jit(solution)/shard_map/ppermute | solution.py:69
  34.6 50.4 %collective-permute-start.9 = (bf16[4,128,128]{2,1,0:T(8,128)(2,1)S(1)}, bf16[4,128,128]{2,1,0:T(8,128)(2,1)S(1)}, u32[]{:S(2)}, u32[]{:S(2)}) collective-permute-start(bf16[4,128,128]{2,1,0:T(8,128)(2,1)S(1)} %pad_maximum_fusion.3), channel_id=1, source_target_pairs={{0,16},{8,24},{16,0},{24,8},{1,17},{9,25},{17,1},{25,9},{2,18},{10... | collective-permute-start | bytes 393224 | tf_op jit(solution)/shard_map/ppermute | solution.py:64
  39.7 7.9 %collective-permute-start.4 = (bf16[4,136,128]{2,1,0:T(8,128)(2,1)S(1)}, bf16[4,136,128]{2,1,0:T(8,128)(2,1)S(1)}, u32[]{:S(2)}, u32[]{:S(2)}) collective-permute-start(bf16[4,136,128]{2,1,0:T(8,128)(2,1)S(1)} %pad_maximum_fusion), channel_id=1, source_target_pairs={{0,8},{8,0},{16,24},{24,16},{1,9},{9,1},{17,25},{25,17},{2,10},{10... | collective-permute-start | bytes 417800 | tf_op jit(solution)/shard_map/ppermute | solution.py:64
  40.1 14.7 %collective-permute-start.5 = (bf16[4,136,128]{2,1,0:T(8,128)(2,1)S(1)}, bf16[4,136,128]{2,1,0:T(8,128)(2,1)S(1)}, u32[]{:S(2)}, u32[]{:S(2)}) collective-permute-start(bf16[4,136,128]{2,1,0:T(8,128)(2,1)S(1)} %pad_maximum_fusion.1), channel_id=1, source_target_pairs={{0,16},{8,24},{16,0},{24,8},{1,17},{9,25},{17,1},{25,9},{2,18},{10... | collective-permute-start | bytes 417800 | tf_op jit(solution)/shard_map/ppermute | solution.py:64
  40.7 14.6 %collective-permute-start.6 = (bf16[4,136,128]{2,1,0:T(8,128)(2,1)S(1)}, bf16[4,136,128]{2,1,0:T(8,128)(2,1)S(1)}, u32[]{:S(2)}, u32[]{:S(2)}) collective-permute-start(bf16[4,136,128]{2,1,0:T(8,128)(2,1)S(1)} %pad_maximum_fusion.2), channel_id=1, source_target_pairs={{0,24},{8,16},{16,8},{24,0},{1,25},{9,17},{17,9},{25,1},{2,26},{10... | collective-permute-start | bytes 417800 | tf_op jit(solution)/shard_map/ppermute | solution.py:64
  63.4 5.5 %collective-permute-start = (bf16[16,128,128]{2,1,0:T(8,128)(2,1)S(1)}, bf16[16,128,128]{2,1,0:T(8,128)(2,1)S(1)}, u32[]{:S(2)}, u32[]{:S(2)}) collective-permute-start(bf16[16,128,128]{2,1,0:T(8,128)(2,1)S(1)} %get-tuple-element.32), channel_id=1, source_target_pairs={{0,1},{1,0},{2,3},{3,2},{4,5},{5,4},{6,7},{7,6},{8,9},{9,8},{10,11... | collective-permute-start | bytes 1572872 | tf_op jit(solution)/shard_map/ppermute | solution.py:69
  64.1 10.8 %collective-permute-start.7 = (bf16[16,136,128]{2,1,0:T(8,128)(2,1)}, bf16[16,136,128]{2,1,0:T(8,128)(2,1)S(1)}, u32[]{:S(2)}, u32[]{:S(2)}) collective-permute-start(bf16[16,136,128]{2,1,0:T(8,128)(2,1)} %get-tuple-element.93), channel_id=1, source_target_pairs={{0,1},{1,0},{2,3},{3,2},{4,5},{5,4},{6,7},{7,6},{8,9},{9,8},{10,11... | collective-permute-start | bytes 1671176 | tf_op jit(solution)/shard_map/ppermute | solution.py:69
  64.6 20.4 %collective-permute-start.10 = (bf16[4,128,128]{2,1,0:T(8,128)(2,1)S(1)}, bf16[4,128,128]{2,1,0:T(8,128)(2,1)S(1)}, u32[]{:S(2)}, u32[]{:S(2)}) collective-permute-start(bf16[4,128,128]{2,1,0:T(8,128)(2,1)S(1)} %pad_maximum_fusion.4), channel_id=1, source_target_pairs={{0,24},{8,16},{16,8},{24,0},{1,25},{9,17},{17,9},{25,1},{2,26},{10... | collective-permute-start | bytes 393224 | tf_op jit(solution)/shard_map/ppermute | solution.py:64
  68.1 8.2 %collective-permute-start.11 = (bf16[4,128,128]{2,1,0:T(8,128)(2,1)S(1)}, bf16[4,128,128]{2,1,0:T(8,128)(2,1)S(1)}, u32[]{:S(2)}, u32[]{:S(2)}) collective-permute-start(bf16[4,128,128]{2,1,0:T(8,128)(2,1)S(1)} %pad_maximum_fusion.6), channel_id=1, source_target_pairs={{0,8},{8,0},{16,24},{24,16},{1,9},{9,1},{17,25},{25,17},{2,10},{10... | collective-permute-start | bytes 393224 | tf_op jit(solution)/shard_map/ppermute | solution.py:64
  74.8 1.2 %collective-permute-start.8 = (f32[32,128]{1,0:T(8,128)S(1)}, f32[32,128]{1,0:T(8,128)S(1)}, u32[]{:S(2)}, u32[]{:S(2)}) collective-permute-start(f32[32,128]{1,0:T(8,128)S(1)} %totals.1.refs_0_), channel_id=1, source_target_pairs={{0,1},{1,0},{2,3},{3,2},{4,5},{5,4},{6,7},{7,6},{8,9},{9,8},{10,11... | collective-permute-start | bytes 49160 | tf_op jit(solution)/shard_map/ppermute | solution.py:69
  94.2 4.4 %collective-permute-start.12 = (f32[16,128,128]{2,1,0:T(8,128)S(1)}, f32[16,128,128]{2,1,0:T(8,128)S(1)}, u32[]{:S(2)}, u32[]{:S(2)}) collective-permute-start(f32[16,128,128]{2,1,0:T(8,128)S(1)} %get-tuple-element.42), channel_id=1, source_target_pairs={{0,1},{1,0},{2,3},{3,2},{4,5},{5,4},{6,7},{7,6},{8,9},{9,8},{10,11... | collective-permute-start | bytes 3145736 | tf_op jit(solution)/shard_map/ppermute | solution.py:69
  94.4 6.4 %collective-permute-start.19 = (bf16[2,2,128,128]{3,2,1,0:T(8,128)(2,1)S(1)}, bf16[2,2,128,128]{3,2,1,0:T(8,128)(2,1)S(1)}, u32[]{:S(2)}, u32[]{:S(2)}) collective-permute-start(bf16[2,2,128,128]{3,2,1,0:T(8,128)(2,1)S(1)} %get-tuple-element.52), channel_id=1, source_target_pairs={{0,2},{1,3},{2,0},{3,1},{4,6},{5,7},{6,4},{7,5},{8,10},{9,11},{10,... | collective-permute-start | bytes 393224 | tf_op jit(solution)/shard_map/ppermute | solution.py:69
  95.1 7.5 %collective-permute-start.20 = (bf16[2,2,128,128]{3,2,1,0:T(8,128)(2,1)S(1)}, bf16[2,2,128,128]{3,2,1,0:T(8,128)(2,1)S(1)}, u32[]{:S(2)}, u32[]{:S(2)}) collective-permute-start(bf16[2,2,128,128]{3,2,1,0:T(8,128)(2,1)S(1)} %get-tuple-element.53), channel_id=1, source_target_pairs={{0,4},{1,5},{2,6},{3,7},{4,0},{5,1},{6,2},{7,3},{8,12},{9,13},{10,... | collective-permute-start | bytes 393224 | tf_op jit(solution)/shard_map/ppermute | solution.py:69
  96.5 8.6 %collective-permute-start.21 = (bf16[2,2,128,128]{3,2,1,0:T(8,128)(2,1)S(1)}, bf16[2,2,128,128]{3,2,1,0:T(8,128)(2,1)S(1)}, u32[]{:S(2)}, u32[]{:S(2)}) collective-permute-start(bf16[2,2,128,128]{3,2,1,0:T(8,128)(2,1)S(1)} %get-tuple-element.54), channel_id=1, source_target_pairs={{0,6},{1,7},{2,4},{3,5},{4,2},{5,3},{6,0},{7,1},{8,14},{9,15},{10,... | collective-permute-start | bytes 393224 | tf_op jit(solution)/shard_map/ppermute | solution.py:69
  97.9 9.2 %collective-permute-start.16 = (bf16[2,2,128,128]{3,2,1,0:T(8,128)(2,1)S(1)}, bf16[2,2,128,128]{3,2,1,0:T(8,128)(2,1)S(1)}, u32[]{:S(2)}, u32[]{:S(2)}) collective-permute-start(bf16[2,2,128,128]{3,2,1,0:T(8,128)(2,1)S(1)} %get-tuple-element.48), channel_id=1, source_target_pairs={{0,2},{1,3},{2,0},{3,1},{4,6},{5,7},{6,4},{7,5},{8,10},{9,11},{10,... | collective-permute-start | bytes 393224 | tf_op jit(solution)/shard_map/ppermute | solution.py:69
  98.6 9.5 %collective-permute-start.17 = (bf16[2,2,128,128]{3,2,1,0:T(8,128)(2,1)S(1)}, bf16[2,2,128,128]{3,2,1,0:T(8,128)(2,1)S(1)}, u32[]{:S(2)}, u32[]{:S(2)}) collective-permute-start(bf16[2,2,128,128]{3,2,1,0:T(8,128)(2,1)S(1)} %get-tuple-element.49), channel_id=1, source_target_pairs={{0,4},{1,5},{2,6},{3,7},{4,0},{5,1},{6,2},{7,3},{8,12},{9,13},{10,... | collective-permute-start | bytes 393224 | tf_op jit(solution)/shard_map/ppermute | solution.py:69
  100.8 9.4 %collective-permute-start.18 = (bf16[2,2,128,128]{3,2,1,0:T(8,128)(2,1)S(1)}, bf16[2,2,128,128]{3,2,1,0:T(8,128)(2,1)S(1)}, u32[]{:S(2)}, u32[]{:S(2)}) collective-permute-start(bf16[2,2,128,128]{3,2,1,0:T(8,128)(2,1)S(1)} %get-tuple-element.50), channel_id=1, source_target_pairs={{0,6},{1,7},{2,4},{3,5},{4,2},{5,3},{6,0},{7,1},{8,14},{9,15},{10,... | collective-permute-start | bytes 393224 | tf_op jit(solution)/shard_map/ppermute | solution.py:69
  102.6 9.5 %collective-permute-start.13 = (bf16[1,4,128,128]{3,2,1,0:T(8,128)(2,1)S(1)}, bf16[1,4,128,128]{3,2,1,0:T(8,128)(2,1)S(1)}, u32[]{:S(2)}, u32[]{:S(2)}) collective-permute-start(bf16[1,4,128,128]{3,2,1,0:T(8,128)(2,1)S(1)} %get-tuple-element.44), channel_id=1, source_target_pairs={{0,2},{1,3},{2,0},{3,1},{4,6},{5,7},{6,4},{7,5},{8,10},{9,11},{10,... | collective-permute-start | bytes 393224 | tf_op jit(solution)/shard_map/ppermute | solution.py:69
  105.1 7.0 %collective-permute-start.14 = (bf16[1,4,128,128]{3,2,1,0:T(8,128)(2,1)S(1)}, bf16[1,4,128,128]{3,2,1,0:T(8,128)(2,1)S(1)}, u32[]{:S(2)}, u32[]{:S(2)}) collective-permute-start(bf16[1,4,128,128]{3,2,1,0:T(8,128)(2,1)S(1)} %get-tuple-element.45), channel_id=1, source_target_pairs={{0,4},{1,5},{2,6},{3,7},{4,0},{5,1},{6,2},{7,3},{8,12},{9,13},{10,... | collective-permute-start | bytes 393224 | tf_op jit(solution)/shard_map/ppermute | solution.py:69
  107.1 8.1 %collective-permute-start.15 = (bf16[1,4,128,128]{3,2,1,0:T(8,128)(2,1)S(1)}, bf16[1,4,128,128]{3,2,1,0:T(8,128)(2,1)S(1)}, u32[]{:S(2)}, u32[]{:S(2)}) collective-permute-start(bf16[1,4,128,128]{3,2,1,0:T(8,128)(2,1)S(1)} %get-tuple-element.46), channel_id=1, source_target_pairs={{0,6},{1,7},{2,4},{3,5},{4,2},{5,3},{6,0},{7,1},{8,14},{9,15},{10,... | collective-permute-start | bytes 393224 | tf_op jit(solution)/shard_map/ppermute | solution.py:69
